TPU v7x, 256 devices: a whole 4x4x8 slice. The times are simulated.
256 devices in a mesh: dp: 16 (over y_hi, x, core), expert: 16 (over y_lo, z).
Axes of the slice: x: 4, y: 4 (y_hi: 2, y_lo: 2; y = y_hi * 2 + y_lo), z: 8, core: 2. Of those that a mesh axis runs over, the one named last changes fastest.
Arguments:
- tokens: bfloat16 [32768, 3072], P(('dp', 'expert')), parts along dimension 0, may hold values from -6 to 6
- w_gate: bfloat16 [3072, 8192], P(None, 'expert'), may hold values from -0.109375 to 0.109375
- w_up: bfloat16 [3072, 8192], P(None, 'expert'), may hold values from -0.109375 to 0.109375
- w_down: bfloat16 [8192, 3072], P('expert'), may hold values from -0.0625 to 0.0625
- route_ids: int32 [32768, 2], P(('dp', 'expert')), parts along dimension 0, may hold values from 0 to 7, as said below
- route_prob: float32 [32768], P(('dp', 'expert')), parts along dimension 0, may hold values from 0.5 to 0.95
- slot_index: int32 [32768], P(('dp', 'expert')), parts along dimension 0, may hold values from 0 to 64, as said below
Outputs:
- mixed: bfloat16 [32768, 3072], P(('dp', 'expert')), parts along dimension 0
There are 16 independent parts, one for each index of `dp`. A program takes and returns all parts, laid end to end along the dimension named above; an argument that names none is the same for every part. Nothing has to cross between parts.
Inputs may be any that keep to these rules, and one draw needn't show every extreme that they name: `route_ids`: each row names two different experts. `slot_index`: a token of whose two experts one is expert 0 holds its rank, in row order, among the tokens of its device that name expert 0; every other token holds 64. At most 64 of one device's 128 tokens name expert 0, and some device has exactly 64; the router's capacity of 64 tokens for expert 0 is counted over each aligned pair of 256 tokens (blocks 2k and 2k + 1) and is always filled, so those two devices have exactly 64 such tokens together.
All inputs are finite; a program needn't handle non-finite values.
Results may differ from a plain program's by a relative error of at most 0.023.
Values may be sent and summed in bfloat16 or wider, within the bound.
No kernel may reach another device: no remote copies, remote signals or barrier semaphores. Data moves between devices by JAX's collectives and lax.ppermute only.
A program may use at most 128 MiB of HBM per device.

v0:
```python
import jax
import jax.numpy as jnp
from jax import lax
from jax.sharding import PartitionSpec as P


def shards(tokens, w_gate, w_up, w_down, route_ids, route_prob, slot_index):
    local_count = tokens.shape[0]
    capacity = local_count // 2
    share = jnp.where(
        route_ids[:, 0] == 0, route_prob, jnp.where(route_ids[:, 1] == 0, 1.0 - route_prob, 0.0)
    )
    share = jnp.where(slot_index < capacity, share, 0.0)
    picker = slot_index[None, :] == jnp.arange(capacity, dtype=jnp.int32)[:, None]
    picker_half = picker.astype(jnp.bfloat16)
    source = jnp.dot(picker_half, tokens, preferred_element_type=jnp.float32).astype(jnp.bfloat16)
    row_share = jnp.dot(picker.astype(jnp.float32), share, precision=lax.Precision.HIGHEST)
    block = lax.all_gather(source, "expert", axis=0, tiled=True)
    gate = jnp.dot(block, w_gate, preferred_element_type=jnp.float32)
    up = jnp.dot(block, w_up, preferred_element_type=jnp.float32)
    hidden = (jax.nn.silu(gate) * up).astype(jnp.bfloat16)
    partial_value = jnp.dot(hidden, w_down, preferred_element_type=jnp.float32).astype(jnp.bfloat16)
    partial_value = lax.optimization_barrier(partial_value)
    terms = partial_value.astype(jnp.float32)
    down = lax.psum_scatter(
        terms.astype(jnp.bfloat16), "expert", scatter_dimension=0, tiled=True
    ).astype(jnp.float32)
    scaled = (row_share[:, None] * down).astype(jnp.bfloat16)
    placed = jnp.einsum("cr,cd->rd", picker_half, scaled, preferred_element_type=jnp.float32)
    return placed.astype(jnp.bfloat16)


def solution(mesh):
    return jax.shard_map(
        shards,
        mesh=mesh,
        in_specs=(
            P(("dp", "expert"), None),
            P(None, "expert"),
            P(None, "expert"),
            P("expert", None),
            P(("dp", "expert"), None),
            P(("dp", "expert")),
            P(("dp", "expert")),
        ),
        out_specs=P(("dp", "expert"), None),
        check_vma=False,
    )
```

profile of v0, /device:TPU:26, one launch (start us, length us, event | category | flops | bytes accessed | tf_op | source)
XLA Modules:
  0.0 207.6 jit_solution(16924911761300009242)
XLA Ops:
  6.5 0.0 copy-start
  6.5 0.0 all-gather.2.cloned.1.call-start
  6.5 2.3 %convolution_convert_fusion.2 = bf16[64,3072]{1,0:T(8,128)(2,1)} fusion(bf16[128,3072]{1,0:T(8,128)(2,1)} %param.7, s32[128]{0:T(128)} %param.13), kind=kOutput, calls=%fused_computation.2 | convolution fusion | flops 50536448 | bytes 1180160 | tf_op jit(solution)/shard_map/dot_general | solution.py:16
  8.8 0.0 all-gather.2.cloned.1.call-update
  8.9 0.0 reduce-scatter.2.cloned.1.call-start
  8.9 85.0 %all-gather.2.cloned.1.call-done = bf16[1024,3072]{1,0:T(8,128)(2,1)} async-done(((bf16[64,3072]{1,0:T(8,128)(2,1)}), bf16[1024,3072]{1,0:T(8,128)(2,1)}) %all-gather.2.cloned.1.call-update) | async-done | bytes 6291472 | tf_op jit(solution)/shard_map/all_gather | solution.py:18
  94.0 8.4 %fusion.18 = f32[1024,512]{1,0:T(8,128)} fusion(bf16[1024,3072]{1,0:T(8,128)(2,1)} %all-gather.2.cloned.1.call-done, bf16[3072,512]{1,0:T(8,128)(2,1)} %param.8), kind=kOutput, calls=%fused_computation.27 | convolution fusion | flops 3221225472 | bytes 11534336 | tf_op jit(solution)/shard_map/dot_general | solution.py:19
  102.4 0.0 copy-done
  102.4 11.9 %convolution_convert_fusion = bf16[1024,3072]{1,0:T(8,128)(2,1)} fusion(bf16[512,3072]{1,0:T(8,128)(2,1)S(1)} %copy-done, f32[1024,512]{1,0:T(8,128)} %fusion.18, bf16[1024,3072]{1,0:T(8,128)(2,1)} %all-gather.2.cloned.1.call-done, bf16[3072,512]{1,0:T(8,128)(2,1)} %param.9), kind=kOutput, calls=%fused_computation | convolution fusion | flops 6448742400 | bytes 20971520 | tf_op jit(solution)/shard_map/dot_general | solution.py:22
  114.3 0.0 copy-start.1
  114.3 0.0 copy-start.2
  114.3 0.0 copy-start.3
  114.3 0.0 reduce-scatter.2.cloned.1.call-update
  114.4 0.6 copy-done.1
  115.0 0.0 copy-done.2
  115.0 0.0 copy-done.3
  115.0 0.1 convolution_bitcast_fusion
  115.1 83.3 %reduce-scatter.2.cloned.1.call-done = bf16[64,3072]{1,0:T(8,128)(2,1)} async-done(((bf16[1024,3072]{1,0:T(8,128)(2,1)}), bf16[64,3072]{1,0:T(8,128)(2,1)}) %reduce-scatter.2.cloned.1.call-update) | async-done | bytes 393232 | tf_op jit(solution)/shard_map/reduce_scatter | solution.py:25
  198.4 2.3 %convolution_convert_fusion.1 = bf16[128,3072]{1,0:T(8,128)(2,1)} fusion(bf16[64,3072]{1,0:T(8,128)(2,1)} %reduce-scatter.2.cloned.1.call-done, f32[64]{0:T(128)S(1)} %convolution_bitcast_fusion, s32[128]{0:T(128)S(1)} %copy-done.1), kind=kOutput, calls=%fused_computation.1 | convolution fusion | flops 51322880 | bytes 1180416 | tf_op jit(solution)/shard_map/cr,cd->rd/dot_general | solution.py:29
Async XLA Ops:
  6.5 95.9 %copy-start = (bf16[512,3072]{1,0:T(8,128)(2,1)S(1)}, bf16[512,3072]{1,0:T(8,128)(2,1)}, u32[]{:S(2)}) copy-start(bf16[512,3072]{1,0:T(8,128)(2,1)} %param.10) | copy-start | bytes 9437188
  6.5 87.4 %all-gather.2.cloned.1.call-start = ((), (), s32[]{:S(2)}) async-start(), calls=%async_computation.1 | async-start | bytes 6684672 | tf_op jit(solution)/shard_map/all_gather | solution.py:18
  8.9 189.5 %reduce-scatter.2.cloned.1.call-start = ((), (), s32[]{:S(2)}) async-start(), calls=%async_computation.2 | async-start | bytes 6684672 | tf_op jit(solution)/shard_map/reduce_scatter | solution.py:25
  114.3 0.7 copy-start.1
  114.3 0.7 copy-start.2
  114.3 0.7 copy-start.3
Sparse Core Ops, SparseCore 0:
  9.1 84.7 all-gather.1
  114.5 83.8 reduce-scatter.1
where the time goes:
time: 208 us
  waiting for transfers between devices  168 us (81%)
  matrix products  25.1 us (12%)
  between operations  13.4 us (6%)
    all_gather x1, waiting for transfers between devices, shards(): block = lax.all_gather(source, 'expert', axis=0, tiled=True)  85 us
    reduce_scatter x1, waiting for transfers between devices, shards(): lax.psum_scatter(terms.astype(jnp.bfloat16), 'expert', scatter_dimension=...  83.3 us
    dot_general x1, matrix products, shards(): jnp.dot(hidden, w_down, preferred_element_type=jnp.float32)  11.9 us
    dot_general x1, matrix products, shards(): gate = jnp.dot(block, w_gate, preferred_element_type=jnp.float32)  8.44 us
  transfers between devices with their start and end apart: 2, of which 2 were waited for; matrix products, arithmetic and copies ran while one was open for 0% of the time, Pallas kernels for 0%

commit v1 on v0

v1 whole, which is shorter than its diff:
```python
import jax
import jax.numpy as jnp
from jax import lax
from jax.sharding import Mesh, PartitionSpec as P

AXES = ("y_hi", "x", "core", "y_lo", "z")
SIZES = (2, 4, 2, 2, 8)
NZ = 8
NY = 4


def along_z(value, step):
    return lax.ppermute(value, "z", [(i, (i + step) % NZ) for i in range(NZ)])


def along_y(value, step):
    def index(y, core):
        return ((y // 2) * 2 + core) * 2 + y % 2

    pairs = [
        (index(y, core), index((y + (step if core == 0 else -step)) % NY, core)) for y in range(NY) for core in range(2)
    ]
    return lax.ppermute(value, ("y_hi", "core", "y_lo"), pairs)


def swap_pair(value):
    return lax.ppermute(value, "z", [(i, i ^ 1) for i in range(NZ)])


def expert(rows, w_gate, w_up, w_down):
    gate = jnp.dot(rows, w_gate, preferred_element_type=jnp.float32)
    up = jnp.dot(rows, w_up, preferred_element_type=jnp.float32)
    hidden = (jax.nn.silu(gate) * up).astype(jnp.bfloat16)
    return jnp.dot(hidden, w_down, preferred_element_type=jnp.float32).astype(jnp.bfloat16)


def total(*terms):
    value = terms[0].astype(jnp.float32)
    for term in terms[1:]:
        value = value + term.astype(jnp.float32)
    return value.astype(jnp.bfloat16)


together = lax.optimization_barrier


def shards(tokens, w_gate, w_up, w_down, route_ids, route_prob, slot_index):
    capacity = tokens.shape[0] // 2
    half = capacity // 2
    quarter = half // 2
    share = jnp.where(
        route_ids[:, 0] == 0, route_prob, jnp.where(route_ids[:, 1] == 0, 1.0 - route_prob, 0.0)
    )
    share = jnp.where(slot_index < capacity, share, 0.0)

    odd = lax.axis_index("z") % 2
    row = jnp.where(odd == 1, capacity - 1 - slot_index, slot_index)
    row = jnp.where(slot_index < capacity, row, -capacity)
    kept_row = row - odd * half
    sent_row = row - (1 - odd) * half
    lanes = jnp.arange(half, dtype=jnp.int32)[:, None]
    keep = (kept_row[None, :] == lanes).astype(jnp.bfloat16)
    send = (sent_row[None, :] == lanes).astype(jnp.bfloat16)
    arrived = swap_pair(jnp.dot(send, tokens, preferred_element_type=jnp.float32).astype(jnp.bfloat16))
    kept = jnp.dot(keep, tokens, preferred_element_type=jnp.float32).astype(jnp.bfloat16)
    own = arrived + kept

    up1, down1 = along_z(own, 1), along_z(own, -1)
    up1, down1 = together((up1, down1))
    up2, down2 = along_z(up1, 1), along_z(down1, -1)
    y1 = along_y(jnp.concatenate([own, up1, down1]), 1)
    up2, down2 = together((up2, down2))
    up3, down3 = along_z(up2, 1), along_z(down2, -1)
    y2 = along_y(jnp.concatenate([up2, down2]), 1)
    up3, down3, y1 = together((up3, down3, y1))
    up4, down4 = along_z(up3[:quarter], 1), along_z(down3[quarter:], -1)
    y3 = along_y(jnp.concatenate([up3, down3]), 1)
    up4, down4, y2 = together((up4, down4, y2))
    y4 = along_y(jnp.concatenate([up4, down4]), 1)

    mine = jnp.concatenate([own, up1, down1, up2, down2, up3, down3, up4, down4])
    mine_out = expert(mine, w_gate, w_up, w_down)
    mine_out, y4 = together((mine_out, y4))
    theirs = jnp.concatenate([y1, y2, y3, y4])
    theirs_out = expert(theirs, w_gate, w_up, w_down)

    def piece(value, c, count=1):
        return value[c * half : (c + count) * half]

    b4 = along_y(piece(theirs_out, 7), -1)
    t4 = total(piece(mine_out, 7), b4)
    b3 = along_y(piece(theirs_out, 5, 2), -1)
    f_down, f_up = along_z(t4[:quarter], -1), along_z(t4[quarter:], 1)
    f_down, f_up, b3 = together((f_down, f_up, b3))
    zero = jnp.zeros_like(f_down)
    f_down, f_up = jnp.concatenate([f_down, zero]), jnp.concatenate([zero, f_up])
    t_down = total(piece(mine_out, 5), b3[:half], f_down)
    t_up = total(piece(mine_out, 6), b3[half:], f_up)
    t_down, t_up = together((t_down, t_up))
    b2 = along_y(piece(theirs_out, 3, 2), -1)
    f_down, f_up = along_z(t_down, -1), along_z(t_up, 1)
    f_down, f_up, b2 = together((f_down, f_up, b2))
    t_down = total(piece(mine_out, 3), b2[:half], f_down)
    t_up = total(piece(mine_out, 4), b2[half:], f_up)
    t_down, t_up = together((t_down, t_up))
    b1 = along_y(piece(theirs_out, 0, 3), -1)
    f_down, f_up = along_z(t_down, -1), along_z(t_up, 1)
    f_down, f_up, b1 = together((f_down, f_up, b1))
    t_down = total(piece(mine_out, 1), b1[half : 2 * half], f_down)
    t_up = total(piece(mine_out, 2), b1[2 * half :], f_up)
    t_down, t_up = together((t_down, t_up))
    f_down, f_up = along_z(t_down, -1), along_z(t_up, 1)
    down_own = total(piece(mine_out, 0), b1[:half], f_down, f_up)

    down_other = swap_pair(down_own)
    placed = jnp.einsum("cr,cd->rd", keep, down_own, preferred_element_type=jnp.float32)
    placed = placed + jnp.einsum("cr,cd->rd", send, down_other, preferred_element_type=jnp.float32)
    return (share[:, None] * placed).astype(jnp.bfloat16)


def solution(mesh):
    fine = Mesh(mesh.devices.reshape(SIZES), AXES)
    every = ("y_hi", "x", "core", "y_lo", "z")
    group = ("y_lo", "z")
    return jax.shard_map(
        shards,
        mesh=fine,
        in_specs=(
            P(every, None),
            P(None, group),
            P(None, group),
            P(group, None),
            P(every, None),
            P(every),
            P(every),
        ),
        out_specs=P(every, None),
        check_vma=False,
    )
```

time: 208 us -> 115 us (0.55)
  waiting for transfers between devices: 168 us -> 49.2 us
  starting transfers between devices: 0.04 us -> 29.9 us
  between operations: 13.4 us -> 0.26 us
  local copies, waits for them, and re-layouts: 0.67 us -> 9.2 us
  matrix products: 25.1 us -> 21.5 us
  other arithmetic: 0 us -> 2.91 us
    all_gather x1 -> x0, waiting for transfers between devices: 85 us -> none  [shards(): block = lax.all_gather(source, 'expert', axis=0, tiled=True)]
    reduce_scatter x1 -> x0, waiting for transfers between devices: 83.3 us -> none  [shards(): lax.psum_scatter(terms.astype(jnp.bfloat16), 'expert', scatter_dimension=...]
    ppermute x0 -> x26, waiting for transfers between devices: none -> 49.2 us  [the longest x16 29.9 us: along_z(): return lax.ppermute(value, 'z', [(i, (i + step) % NZ) for i in range(NZ)])]
    ppermute x0 -> x26, starting transfers between devices: none -> 29.9 us  [the longest x16 24.3 us: along_z(): return lax.ppermute(value, 'z', [(i, (i + step) % NZ) for i in range(NZ)])]
    dot_general x5 -> x8, matrix products: 25.1 us -> 21.5 us  [the longest x2 11 us: expert(): jnp.dot(hidden, w_down, preferred_element_type=jnp.float32)]
    unnamed x8 -> x24, local copies, waits for them, and re-layouts: 0.67 us -> 4.23 us
    slice x0 -> x6, local copies, waits for them, and re-layouts: none -> 3.36 us  [the longest x3 3.33 us: piece(): return value[c * half:(c + count) * half]]
  transfers between devices with their start and end apart: 2 -> 26, of which waited for: 2 -> 17; matrix products, arithmetic and copies ran while one was open for 0% -> 12% of each run, Pallas kernels for 0% -> 0%
where the time goes in v1:
time: 115 us; the launch traced here: 113 us
  waiting for transfers between devices  49.2 us (43%)
  starting transfers between devices  29.9 us (26%)
  matrix products  21.5 us (19%)
  local copies, waits for them, and re-layouts  9.2 us (8%)
  other arithmetic  2.91 us (3%)
    ppermute x16, waiting for transfers between devices, along_z(): return lax.ppermute(value, 'z', [(i, (i + step) % NZ) for i in range(NZ)])  29.9 us
    ppermute x16, starting transfers between devices, along_z(): return lax.ppermute(value, 'z', [(i, (i + step) % NZ) for i in range(NZ)])  24.3 us
    dot_general x2, matrix products, expert(): jnp.dot(hidden, w_down, preferred_element_type=jnp.float32)  11 us
    ppermute x2, waiting for transfers between devices, swap_pair(): return lax.ppermute(value, 'z', [(i, i ^ 1) for i in range(NZ)])  10.5 us
    ppermute x8, waiting for transfers between devices, along_y(): return lax.ppermute(value, ('y_hi', 'core', 'y_lo'), pairs)  8.8 us
    dot_general x2, matrix products, expert(): gate = jnp.dot(rows, w_gate, preferred_element_type=jnp.float32)  5.9 us
    unnamed x24, local copies, waits for them, and re-layouts  4.23 us
    ppermute x8, starting transfers between devices, along_y(): return lax.ppermute(value, ('y_hi', 'core', 'y_lo'), pairs)  3.43 us
  transfers between devices with their start and end apart: 26, of which 17 were waited for; matrix products, arithmetic and copies ran while one was open for 12% of the time, Pallas kernels for 0%

profile of v1, /device:TPU:26, one launch (start us, length us, event | category | flops | bytes accessed | tf_op | source)
XLA Modules:
  0.0 113.0 jit_solution(9506384602817356129)
XLA Ops:
  2.3 2.0 %collective-permute-start = (bf16[32,3072]{1,0:T(8,128)(2,1)S(1)}, bf16[32,3072]{1,0:T(8,128)(2,1)S(1)}, u32[]{:S(2)}, u32[]{:S(2)}) collective-permute-start(bf16[32,3072]{1,0:T(8,128)(2,1)S(1)} %convolution_convert_fusion.3), channel_id=1, source_target_pairs={{0,1},{1,0},{2,3},{3,2},{4,5},{5,4},{6,7},{7,6},{8,9},{9,8},{10,11... | collective-permute-start | bytes 589832 | tf_op jit(solution)/shard_map/ppermute | solution.py:27
  4.3 4.9 %collective-permute-done = bf16[32,3072]{1,0:T(8,128)(2,1)S(1)} collective-permute-done((bf16[32,3072]{1,0:T(8,128)(2,1)S(1)}, bf16[32,3072]{1,0:T(8,128)(2,1)S(1)}, u32[]{:S(2)}, u32[]{:S(2)}) %collective-permute-start) | collective-permute-done | bytes 196640 | tf_op jit(solution)/shard_map/ppermute | solution.py:27
  10.6 1.8 %collective-permute-start.1 = (bf16[32,3072]{1,0:T(8,128)(2,1)S(1)}, bf16[32,3072]{1,0:T(8,128)(2,1)S(1)}, u32[]{:S(2)}, u32[]{:S(2)}) collective-permute-start(bf16[32,3072]{1,0:T(8,128)(2,1)S(1)} %get-tuple-element.72), channel_id=1, source_target_pairs={{0,1},{1,2},{2,3},{3,4},{4,5},{5,6},{6,7},{7,0},{8,9},{9,10},{10,1... | collective-permute-start | bytes 589832 | tf_op jit(solution)/shard_map/ppermute | solution.py:13
  12.4 4.0 %collective-permute-start.2 = (bf16[32,3072]{1,0:T(8,128)(2,1)S(1)}, bf16[32,3072]{1,0:T(8,128)(2,1)S(1)}, u32[]{:S(2)}, u32[]{:S(2)}) collective-permute-start(bf16[32,3072]{1,0:T(8,128)(2,1)S(1)} %get-tuple-element.72), channel_id=1, source_target_pairs={{0,7},{1,0},{2,1},{3,2},{4,3},{5,4},{6,5},{7,6},{8,15},{9,8},{10,9... | collective-permute-start | bytes 589832 | tf_op jit(solution)/shard_map/ppermute | solution.py:13
  16.5 3.9 %collective-permute-done.1 = bf16[32,3072]{1,0:T(8,128)(2,1)S(1)} collective-permute-done((bf16[32,3072]{1,0:T(8,128)(2,1)S(1)}, bf16[32,3072]{1,0:T(8,128)(2,1)S(1)}, u32[]{:S(2)}, u32[]{:S(2)}) %collective-permute-start.1) | collective-permute-done | bytes 196640 | tf_op jit(solution)/shard_map/ppermute | solution.py:13
  20.4 3.2 %collective-permute-start.4 = (bf16[32,3072]{1,0:T(8,128)(2,1)S(1)}, bf16[32,3072]{1,0:T(8,128)(2,1)S(1)}, u32[]{:S(2)}, u32[]{:S(2)}) collective-permute-start(bf16[32,3072]{1,0:T(8,128)(2,1)S(1)} %collective-permute-done.2), channel_id=1, source_target_pairs={{0,7},{1,0},{2,1},{3,2},{4,3},{5,4},{6,5},{7,6},{8,15},{9,8},{10,9... | collective-permute-start | bytes 589832 | tf_op jit(solution)/shard_map/ppermute | solution.py:13
  24.0 3.3 %collective-permute-done.3 = bf16[32,3072]{1,0:T(8,128)(2,1)S(1)} collective-permute-done((bf16[32,3072]{1,0:T(8,128)(2,1)S(1)}, bf16[32,3072]{1,0:T(8,128)(2,1)S(1)}, u32[]{:S(2)}, u32[]{:S(2)}) %collective-permute-start.3) | collective-permute-done | bytes 196640 | tf_op jit(solution)/shard_map/ppermute | solution.py:13
  27.3 2.6 %collective-permute-start.5 = (bf16[32,3072]{1,0:T(8,128)(2,1)S(1)}, bf16[32,3072]{1,0:T(8,128)(2,1)S(1)}, u32[]{:S(2)}, u32[]{:S(2)}) collective-permute-start(bf16[32,3072]{1,0:T(8,128)(2,1)S(1)} %collective-permute-done.3), channel_id=1, source_target_pairs={{0,1},{1,2},{2,3},{3,4},{4,5},{5,6},{6,7},{7,0},{8,9},{9,10},{10,1... | collective-permute-start | bytes 589832 | tf_op jit(solution)/shard_map/ppermute | solution.py:13
  30.9 3.3 %collective-permute-done.5 = bf16[32,3072]{1,0:T(8,128)(2,1)S(1)} collective-permute-done((bf16[32,3072]{1,0:T(8,128)(2,1)S(1)}, bf16[32,3072]{1,0:T(8,128)(2,1)S(1)}, u32[]{:S(2)}, u32[]{:S(2)}) %collective-permute-start.5) | collective-permute-done | bytes 196640 | tf_op jit(solution)/shard_map/ppermute | solution.py:13
  36.4 2.0 %collective-permute-start.8 = (bf16[16,3072]{1,0:T(8,128)(2,1)S(1)}, bf16[16,3072]{1,0:T(8,128)(2,1)S(1)}, u32[]{:S(2)}, u32[]{:S(2)}) collective-permute-start(bf16[16,3072]{1,0:T(8,128)(2,1)S(1)} %slice.77), channel_id=1, source_target_pairs={{0,1},{1,2},{2,3},{3,4},{4,5},{5,6},{6,7},{7,0},{8,9},{9,10},{10,1... | collective-permute-start | bytes 294920 | tf_op jit(solution)/shard_map/ppermute | solution.py:13
  46.7 5.5 %convolution_convert_fusion.1 = bf16[256,3072]{1,0:T(8,128)(2,1)} fusion(bf16[512,3072]{1,0:T(8,128)(2,1)S(1)} %copy-done, bf16[256,3072]{1,0:T(8,128)(2,1)} %copy-done.2, bf16[3072,512]{1,0:T(8,128)(2,1)} %param.9, f32[256,512]{1,0:T(8,128)} %fusion.22), kind=kOutput, calls=%fused_computation.1 | convolution fusion | flops 1612185600 | bytes 9961472 | tf_op jit(solution)/shard_map/dot_general | solution.py:34
  56.4 4.1 %fusion.23 = f32[256,512]{1,0:T(8,128)} fusion(bf16[256,3072]{1,0:T(8,128)(2,1)} %constant_dynamic-update-slice_fusion.9, bf16[3072,512]{1,0:T(8,128)(2,1)} %param.8), kind=kOutput, calls=%fused_computation.63 | convolution fusion | flops 805306368 | bytes 5242880 | tf_op jit(solution)/shard_map/dot_general | solution.py:31
  60.6 5.5 %convolution_convert_fusion = bf16[256,3072]{1,0:T(8,128)(2,1)} fusion(bf16[512,3072]{1,0:T(8,128)(2,1)S(1)} %copy-done, f32[256,512]{1,0:T(8,128)} %fusion.23, bf16[256,3072]{1,0:T(8,128)(2,1)} %constant_dynamic-update-slice_fusion.9, bf16[3072,512]{1,0:T(8,128)(2,1)} %param.9), kind=kOutput, calls=%fused_computation | convolution fusion | flops 1612185600 | bytes 9961472 | tf_op jit(solution)/shard_map/dot_general | solution.py:34
  70.3 3.7 %collective-permute-done.13 = bf16[32,3072]{1,0:T(8,128)(2,1)S(1)} collective-permute-done((bf16[32,3072]{1,0:T(8,128)(2,1)S(1)}, bf16[32,3072]{1,0:T(8,128)(2,1)S(1)}, u32[]{:S(2)}, u32[]{:S(2)}) %collective-permute-start.13) | collective-permute-done | bytes 196640 | tf_op jit(solution)/shard_map/ppermute | solution.py:23
  74.2 2.5 %collective-permute-start.14 = (bf16[16,3072]{1,0:T(8,128)(2,1)S(1)}, bf16[16,3072]{1,0:T(8,128)(2,1)S(1)}, u32[]{:S(2)}, u32[]{:S(2)}) collective-permute-start(bf16[16,3072]{1,0:T(8,128)(2,1)S(1)} %get-tuple-element.68), channel_id=1, source_target_pairs={{0,7},{1,0},{2,1},{3,2},{4,3},{5,4},{6,5},{7,6},{8,15},{9,8},{10,9... | collective-permute-start | bytes 294920 | tf_op jit(solution)/shard_map/ppermute | solution.py:13
  76.6 2.7 %collective-permute-done.14 = bf16[16,3072]{1,0:T(8,128)(2,1)S(1)} collective-permute-done((bf16[16,3072]{1,0:T(8,128)(2,1)S(1)}, bf16[16,3072]{1,0:T(8,128)(2,1)S(1)}, u32[]{:S(2)}, u32[]{:S(2)}) %collective-permute-start.14) | collective-permute-done | bytes 98336 | tf_op jit(solution)/shard_map/ppermute | solution.py:13
  79.4 3.1 %collective-permute-done.15 = bf16[16,3072]{1,0:T(8,128)(2,1)S(1)} collective-permute-done((bf16[16,3072]{1,0:T(8,128)(2,1)S(1)}, bf16[16,3072]{1,0:T(8,128)(2,1)S(1)}, u32[]{:S(2)}, u32[]{:S(2)}) %collective-permute-start.15) | collective-permute-done | bytes 98336 | tf_op jit(solution)/shard_map/ppermute | solution.py:13
  82.7 2.0 %collective-permute-start.18 = (bf16[32,3072]{1,0:T(8,128)(2,1)S(1)}, bf16[32,3072]{1,0:T(8,128)(2,1)S(1)}, u32[]{:S(2)}, u32[]{:S(2)}) collective-permute-start(bf16[32,3072]{1,0:T(8,128)(2,1)S(1)} %get-tuple-element.48), channel_id=1, source_target_pairs={{0,1},{1,2},{2,3},{3,4},{4,5},{5,6},{6,7},{7,0},{8,9},{9,10},{10,1... | collective-permute-start | bytes 589832 | tf_op jit(solution)/shard_map/ppermute | solution.py:13
  85.9 2.4 %collective-permute-done.17 = bf16[32,3072]{1,0:T(8,128)(2,1)S(1)} collective-permute-done((bf16[32,3072]{1,0:T(8,128)(2,1)S(1)}, bf16[32,3072]{1,0:T(8,128)(2,1)S(1)}, u32[]{:S(2)}, u32[]{:S(2)}) %collective-permute-start.17) | collective-permute-done | bytes 196640 | tf_op jit(solution)/shard_map/ppermute | solution.py:13
  90.1 1.8 %collective-permute-start.21 = (bf16[32,3072]{1,0:T(8,128)(2,1)S(1)}, bf16[32,3072]{1,0:T(8,128)(2,1)S(1)}, u32[]{:S(2)}, u32[]{:S(2)}) collective-permute-start(bf16[32,3072]{1,0:T(8,128)(2,1)S(1)} %get-tuple-element.53), channel_id=1, source_target_pairs={{0,1},{1,2},{2,3},{3,4},{4,5},{5,6},{6,7},{7,0},{8,9},{9,10},{10,1... | collective-permute-start | bytes 589832 | tf_op jit(solution)/shard_map/ppermute | solution.py:13
  91.9 5.0 %collective-permute-done.22 = bf16[96,3072]{1,0:T(8,128)(2,1)S(1)} collective-permute-done((bf16[96,3072]{1,0:T(8,128)(2,1)S(1)}, bf16[96,3072]{1,0:T(8,128)(2,1)S(1)}, u32[]{:S(2)}, u32[]{:S(2)}) %collective-permute-start.22) | collective-permute-done | bytes 589856 | tf_op jit(solution)/shard_map/ppermute | solution.py:23
  99.3 3.6 %collective-permute-done.23 = bf16[32,3072]{1,0:T(8,128)(2,1)S(1)} collective-permute-done((bf16[32,3072]{1,0:T(8,128)(2,1)S(1)}, bf16[32,3072]{1,0:T(8,128)(2,1)S(1)}, u32[]{:S(2)}, u32[]{:S(2)}) %collective-permute-start.23) | collective-permute-done | bytes 196640 | tf_op jit(solution)/shard_map/ppermute | solution.py:13
  103.0 2.4 %collective-permute-done.24 = bf16[32,3072]{1,0:T(8,128)(2,1)S(1)} collective-permute-done((bf16[32,3072]{1,0:T(8,128)(2,1)S(1)}, bf16[32,3072]{1,0:T(8,128)(2,1)S(1)}, u32[]{:S(2)}, u32[]{:S(2)}) %collective-permute-start.24) | collective-permute-done | bytes 196640 | tf_op jit(solution)/shard_map/ppermute | solution.py:13
  105.6 5.6 %collective-permute-done.25 = bf16[32,3072]{1,0:T(8,128)(2,1)S(1)} collective-permute-done((bf16[32,3072]{1,0:T(8,128)(2,1)S(1)}, bf16[32,3072]{1,0:T(8,128)(2,1)S(1)}, u32[]{:S(2)}, u32[]{:S(2)}) %collective-permute-start.25) | collective-permute-done | bytes 196640 | tf_op jit(solution)/shard_map/ppermute | solution.py:27
  (79 shorter events, 31.4 us)
Async XLA Ops:
  2.3 6.9 %collective-permute-start = (bf16[32,3072]{1,0:T(8,128)(2,1)S(1)}, bf16[32,3072]{1,0:T(8,128)(2,1)S(1)}, u32[]{:S(2)}, u32[]{:S(2)}) collective-permute-start(bf16[32,3072]{1,0:T(8,128)(2,1)S(1)} %convolution_convert_fusion.3), channel_id=1, source_target_pairs={{0,1},{1,0},{2,3},{3,2},{4,5},{5,4},{6,7},{7,6},{8,9},{9,8},{10,11... | collective-permute-start | bytes 589832 | tf_op jit(solution)/shard_map/ppermute | solution.py:27
  10.6 9.8 %collective-permute-start.1 = (bf16[32,3072]{1,0:T(8,128)(2,1)S(1)}, bf16[32,3072]{1,0:T(8,128)(2,1)S(1)}, u32[]{:S(2)}, u32[]{:S(2)}) collective-permute-start(bf16[32,3072]{1,0:T(8,128)(2,1)S(1)} %get-tuple-element.72), channel_id=1, source_target_pairs={{0,1},{1,2},{2,3},{3,4},{4,5},{5,6},{6,7},{7,0},{8,9},{9,10},{10,1... | collective-permute-start | bytes 589832 | tf_op jit(solution)/shard_map/ppermute | solution.py:13
  12.4 8.0 %collective-permute-start.2 = (bf16[32,3072]{1,0:T(8,128)(2,1)S(1)}, bf16[32,3072]{1,0:T(8,128)(2,1)S(1)}, u32[]{:S(2)}, u32[]{:S(2)}) collective-permute-start(bf16[32,3072]{1,0:T(8,128)(2,1)S(1)} %get-tuple-element.72), channel_id=1, source_target_pairs={{0,7},{1,0},{2,1},{3,2},{4,3},{5,4},{6,5},{7,6},{8,15},{9,8},{10,9... | collective-permute-start | bytes 589832 | tf_op jit(solution)/shard_map/ppermute | solution.py:13
  20.4 6.9 %collective-permute-start.3 = (bf16[32,3072]{1,0:T(8,128)(2,1)S(1)}, bf16[32,3072]{1,0:T(8,128)(2,1)S(1)}, u32[]{:S(2)}, u32[]{:S(2)}) collective-permute-start(bf16[32,3072]{1,0:T(8,128)(2,1)S(1)} %collective-permute-done.1), channel_id=1, source_target_pairs={{0,1},{1,2},{2,3},{3,4},{4,5},{5,6},{6,7},{7,0},{8,9},{9,10},{10,1... | collective-permute-start | bytes 589832 | tf_op jit(solution)/shard_map/ppermute | solution.py:13
  20.4 6.9 %collective-permute-start.4 = (bf16[32,3072]{1,0:T(8,128)(2,1)S(1)}, bf16[32,3072]{1,0:T(8,128)(2,1)S(1)}, u32[]{:S(2)}, u32[]{:S(2)}) collective-permute-start(bf16[32,3072]{1,0:T(8,128)(2,1)S(1)} %collective-permute-done.2), channel_id=1, source_target_pairs={{0,7},{1,0},{2,1},{3,2},{4,3},{5,4},{6,5},{7,6},{8,15},{9,8},{10,9... | collective-permute-start | bytes 589832 | tf_op jit(solution)/shard_map/ppermute | solution.py:13
  23.7 11.9 %collective-permute-start.7 = (bf16[96,3072]{1,0:T(8,128)(2,1)S(1)}, bf16[96,3072]{1,0:T(8,128)(2,1)S(1)}, u32[]{:S(2)}, u32[]{:S(2)}) collective-permute-start(bf16[96,3072]{1,0:T(8,128)(2,1)S(1)} %pad_maximum_fusion), channel_id=1, source_target_pairs={{0,8},{16,152},{8,128},{24,16},{128,136},{144,24},{136,0},{152,144... | collective-permute-start | bytes 1769480 | tf_op jit(solution)/shard_map/ppermute | solution.py:23
  27.3 6.9 %collective-permute-start.5 = (bf16[32,3072]{1,0:T(8,128)(2,1)S(1)}, bf16[32,3072]{1,0:T(8,128)(2,1)S(1)}, u32[]{:S(2)}, u32[]{:S(2)}) collective-permute-start(bf16[32,3072]{1,0:T(8,128)(2,1)S(1)} %collective-permute-done.3), channel_id=1, source_target_pairs={{0,1},{1,2},{2,3},{3,4},{4,5},{5,6},{6,7},{7,0},{8,9},{9,10},{10,1... | collective-permute-start | bytes 589832 | tf_op jit(solution)/shard_map/ppermute | solution.py:13
  29.9 5.7 %collective-permute-start.6 = (bf16[32,3072]{1,0:T(8,128)(2,1)S(1)}, bf16[32,3072]{1,0:T(8,128)(2,1)S(1)}, u32[]{:S(2)}, u32[]{:S(2)}) collective-permute-start(bf16[32,3072]{1,0:T(8,128)(2,1)S(1)} %collective-permute-done.4), channel_id=1, source_target_pairs={{0,7},{1,0},{2,1},{3,2},{4,3},{5,4},{6,5},{7,6},{8,15},{9,8},{10,9... | collective-permute-start | bytes 589832 | tf_op jit(solution)/shard_map/ppermute | solution.py:13
  30.6 10.2 %collective-permute-start.10 = (bf16[64,3072]{1,0:T(8,128)(2,1)S(1)}, bf16[64,3072]{1,0:T(8,128)(2,1)S(1)}, u32[]{:S(2)}, u32[]{:S(2)}) collective-permute-start(bf16[64,3072]{1,0:T(8,128)(2,1)S(1)} %pad_maximum_fusion.1), channel_id=1, source_target_pairs={{0,8},{16,152},{8,128},{24,16},{128,136},{144,24},{136,0},{152,144... | collective-permute-start | bytes 1179656 | tf_op jit(solution)/shard_map/ppermute | solution.py:23
  36.4 5.8 %collective-permute-start.8 = (bf16[16,3072]{1,0:T(8,128)(2,1)S(1)}, bf16[16,3072]{1,0:T(8,128)(2,1)S(1)}, u32[]{:S(2)}, u32[]{:S(2)}) collective-permute-start(bf16[16,3072]{1,0:T(8,128)(2,1)S(1)} %slice.77), channel_id=1, source_target_pairs={{0,1},{1,2},{2,3},{3,4},{4,5},{5,6},{6,7},{7,0},{8,9},{9,10},{10,1... | collective-permute-start | bytes 294920 | tf_op jit(solution)/shard_map/ppermute | solution.py:13
  39.6 13.4 %collective-permute-start.12 = (bf16[64,3072]{1,0:T(8,128)(2,1)}, bf16[64,3072]{1,0:T(8,128)(2,1)}, u32[]{:S(2)}, u32[]{:S(2)}) collective-permute-start(bf16[64,3072]{1,0:T(8,128)(2,1)} %pad_maximum_fusion.2), channel_id=1, source_target_pairs={{0,8},{16,152},{8,128},{24,16},{128,136},{144,24},{136,0},{152,144... | collective-permute-start | bytes 1179656 | tf_op jit(solution)/shard_map/ppermute | solution.py:23
  43.8 9.3 %collective-permute-start.11 = (bf16[32,3072]{1,0:T(8,128)(2,1)}, bf16[32,3072]{1,0:T(8,128)(2,1)}, u32[]{:S(2)}, u32[]{:S(2)}) collective-permute-start(bf16[32,3072]{1,0:T(8,128)(2,1)} %pad_maximum_fusion.3), channel_id=1, source_target_pairs={{0,8},{16,152},{8,128},{24,16},{128,136},{144,24},{136,0},{152,144... | collective-permute-start | bytes 589832 | tf_op jit(solution)/shard_map/ppermute | solution.py:23
  67.1 7.0 %collective-permute-start.13 = (bf16[32,3072]{1,0:T(8,128)(2,1)S(1)}, bf16[32,3072]{1,0:T(8,128)(2,1)S(1)}, u32[]{:S(2)}, u32[]{:S(2)}) collective-permute-start(bf16[32,3072]{1,0:T(8,128)(2,1)S(1)} %slice.100), channel_id=1, source_target_pairs={{0,136},{16,24},{8,0},{24,144},{128,8},{144,152},{136,128},{152,16... | collective-permute-start | bytes 589832 | tf_op jit(solution)/shard_map/ppermute | solution.py:23
  69.5 12.9 %collective-permute-start.16 = (bf16[64,3072]{1,0:T(8,128)(2,1)S(1)}, bf16[64,3072]{1,0:T(8,128)(2,1)S(1)}, u32[]{:S(2)}, u32[]{:S(2)}) collective-permute-start(bf16[64,3072]{1,0:T(8,128)(2,1)S(1)} %get-tuple-element.66), channel_id=1, source_target_pairs={{0,136},{16,24},{8,0},{24,144},{128,8},{144,152},{136,128},{152,16... | collective-permute-start | bytes 1179656 | tf_op jit(solution)/shard_map/ppermute | solution.py:23
  76.6 5.8 %collective-permute-start.15 = (bf16[16,3072]{1,0:T(8,128)(2,1)S(1)}, bf16[16,3072]{1,0:T(8,128)(2,1)S(1)}, u32[]{:S(2)}, u32[]{:S(2)}) collective-permute-start(bf16[16,3072]{1,0:T(8,128)(2,1)S(1)} %get-tuple-element.67), channel_id=1, source_target_pairs={{0,1},{1,2},{2,3},{3,4},{4,5},{5,6},{6,7},{7,0},{8,9},{9,10},{10,1... | collective-permute-start | bytes 294920 | tf_op jit(solution)/shard_map/ppermute | solution.py:13
  76.6 9.3 %collective-permute-start.19 = (bf16[64,3072]{1,0:T(8,128)(2,1)S(1)}, bf16[64,3072]{1,0:T(8,128)(2,1)S(1)}, u32[]{:S(2)}, u32[]{:S(2)}) collective-permute-start(bf16[64,3072]{1,0:T(8,128)(2,1)S(1)} %get-tuple-element.65), channel_id=1, source_target_pairs={{0,136},{16,24},{8,0},{24,144},{128,8},{144,152},{136,128},{152,16... | collective-permute-start | bytes 1179656 | tf_op jit(solution)/shard_map/ppermute | solution.py:23
  82.6 5.7 %collective-permute-start.17 = (bf16[32,3072]{1,0:T(8,128)(2,1)S(1)}, bf16[32,3072]{1,0:T(8,128)(2,1)S(1)}, u32[]{:S(2)}, u32[]{:S(2)}) collective-permute-start(bf16[32,3072]{1,0:T(8,128)(2,1)S(1)} %get-tuple-element.47), channel_id=1, source_target_pairs={{0,7},{1,0},{2,1},{3,2},{4,3},{5,4},{6,5},{7,6},{8,15},{9,8},{10,9... | collective-permute-start | bytes 589832 | tf_op jit(solution)/shard_map/ppermute | solution.py:13
  82.7 7.0 %collective-permute-start.18 = (bf16[32,3072]{1,0:T(8,128)(2,1)S(1)}, bf16[32,3072]{1,0:T(8,128)(2,1)S(1)}, u32[]{:S(2)}, u32[]{:S(2)}) collective-permute-start(bf16[32,3072]{1,0:T(8,128)(2,1)S(1)} %get-tuple-element.48), channel_id=1, source_target_pairs={{0,1},{1,2},{2,3},{3,4},{4,5},{5,6},{6,7},{7,0},{8,9},{9,10},{10,1... | collective-permute-start | bytes 589832 | tf_op jit(solution)/shard_map/ppermute | solution.py:13
  85.8 11.2 %collective-permute-start.22 = (bf16[96,3072]{1,0:T(8,128)(2,1)S(1)}, bf16[96,3072]{1,0:T(8,128)(2,1)S(1)}, u32[]{:S(2)}, u32[]{:S(2)}) collective-permute-start(bf16[96,3072]{1,0:T(8,128)(2,1)S(1)} %slice.105), channel_id=1, source_target_pairs={{0,136},{16,24},{8,0},{24,144},{128,8},{144,152},{136,128},{152,16... | collective-permute-start | bytes 1769480 | tf_op jit(solution)/shard_map/ppermute | solution.py:23
  89.8 7.2 %collective-permute-start.20 = (bf16[32,3072]{1,0:T(8,128)(2,1)S(1)}, bf16[32,3072]{1,0:T(8,128)(2,1)S(1)}, u32[]{:S(2)}, u32[]{:S(2)}) collective-permute-start(bf16[32,3072]{1,0:T(8,128)(2,1)S(1)} %get-tuple-element.52), channel_id=1, source_target_pairs={{0,7},{1,0},{2,1},{3,2},{4,3},{5,4},{6,5},{7,6},{8,15},{9,8},{10,9... | collective-permute-start | bytes 589832 | tf_op jit(solution)/shard_map/ppermute | solution.py:13
  90.1 7.0 %collective-permute-start.21 = (bf16[32,3072]{1,0:T(8,128)(2,1)S(1)}, bf16[32,3072]{1,0:T(8,128)(2,1)S(1)}, u32[]{:S(2)}, u32[]{:S(2)}) collective-permute-start(bf16[32,3072]{1,0:T(8,128)(2,1)S(1)} %get-tuple-element.53), channel_id=1, source_target_pairs={{0,1},{1,2},{2,3},{3,4},{4,5},{5,6},{6,7},{7,0},{8,9},{9,10},{10,1... | collective-permute-start | bytes 589832 | tf_op jit(solution)/shard_map/ppermute | solution.py:13
  97.2 5.7 %collective-permute-start.23 = (bf16[32,3072]{1,0:T(8,128)(2,1)S(1)}, bf16[32,3072]{1,0:T(8,128)(2,1)S(1)}, u32[]{:S(2)}, u32[]{:S(2)}) collective-permute-start(bf16[32,3072]{1,0:T(8,128)(2,1)S(1)} %get-tuple-element.57), channel_id=1, source_target_pairs={{0,7},{1,0},{2,1},{3,2},{4,3},{5,4},{6,5},{7,6},{8,15},{9,8},{10,9... | collective-permute-start | bytes 589832 | tf_op jit(solution)/shard_map/ppermute | solution.py:13
  98.5 6.9 %collective-permute-start.24 = (bf16[32,3072]{1,0:T(8,128)(2,1)S(1)}, bf16[32,3072]{1,0:T(8,128)(2,1)S(1)}, u32[]{:S(2)}, u32[]{:S(2)}) collective-permute-start(bf16[32,3072]{1,0:T(8,128)(2,1)S(1)} %get-tuple-element.58), channel_id=1, source_target_pairs={{0,1},{1,2},{2,3},{3,4},{4,5},{5,6},{6,7},{7,0},{8,9},{9,10},{10,1... | collective-permute-start | bytes 589832 | tf_op jit(solution)/shard_map/ppermute | solution.py:13
  105.5 5.8 %collective-permute-start.25 = (bf16[32,3072]{1,0:T(8,128)(2,1)S(1)}, bf16[32,3072]{1,0:T(8,128)(2,1)S(1)}, u32[]{:S(2)}, u32[]{:S(2)}) collective-permute-start(bf16[32,3072]{1,0:T(8,128)(2,1)S(1)} %add_convert_fusion), channel_id=1, source_target_pairs={{0,1},{1,0},{2,3},{3,2},{4,5},{5,4},{6,7},{7,6},{8,9},{9,8},{10,11... | collective-permute-start | bytes 589832 | tf_op jit(solution)/shard_map/ppermute | solution.py:27
  (9 other events, 122.5 us)

commit v2 on v1

v2 whole, which is shorter than its diff:
```python
import functools

import jax
import jax.numpy as jnp
from jax import lax
from jax.experimental import pallas as pl
from jax.experimental.pallas import tpu as pltpu
from jax.sharding import Mesh, PartitionSpec as P

AXES = ("y_hi", "x", "core", "y_lo", "z")
SIZES = (2, 4, 2, 2, 8)
NZ = 8
NY = 4


def along_z(value, step):
    def index(core, z):
        return core * NZ + z

    pairs = [
        (index(core, z), index(core, (z + (step if core == 0 else -step)) % NZ)) for core in range(2) for z in range(NZ)
    ]
    return lax.ppermute(value, ("core", "z"), pairs)


def along_y(value, step):
    def index(y, core):
        return ((y // 2) * 2 + core) * 2 + y % 2

    pairs = [
        (index(y, core), index((y + (step if core == 0 else -step)) % NY, core)) for y in range(NY) for core in range(2)
    ]
    return lax.ppermute(value, ("y_hi", "core", "y_lo"), pairs)


def swap_pair(value):
    return lax.ppermute(value, "z", [(i, i ^ 1) for i in range(NZ)])


def diagonal(value, step_y, step_z):
    def index(y, core, z):
        return (((y // 2) * 2 + core) * 2 + y % 2) * NZ + z

    pairs = [
        (index(y, core, z), index((y + (step_y if core == 0 else -step_y)) % NY, core, (z + (step_z if core == 0 else -step_z)) % NZ))
        for y in range(NY)
        for core in range(2)
        for z in range(NZ)
    ]
    return lax.ppermute(value, ("y_hi", "core", "y_lo", "z"), pairs)


def expert_kernel(count, *refs):
    pieces, (w_gate, w_up, w_down) = refs[:count], refs[count : count + 3]
    outs, (rows, hidden) = refs[count + 3 : 2 * count + 3], refs[2 * count + 3 :]
    at = 0
    for piece in pieces:
        rows[pl.ds(at, piece.shape[0]), :] = piece[...]
        at += piece.shape[0]
    inner, width = w_down.shape
    for start in range(0, inner, 256):
        stop = min(start + 256, inner)
        gate = jnp.dot(rows[...], w_gate[:, start:stop], preferred_element_type=jnp.float32)
        up = jnp.dot(rows[...], w_up[:, start:stop], preferred_element_type=jnp.float32)
        hidden[:, start:stop] = (gate / (1.0 + jnp.exp(-gate)) * up).astype(hidden.dtype)
    for start in range(0, width, 512):
        stop = min(start + 512, width)
        part = jnp.dot(hidden[...], w_down[:, start:stop], preferred_element_type=jnp.float32)
        part = part.astype(hidden.dtype)
        at = 0
        for out in outs:
            out[:, start:stop] = part[at : at + out.shape[0]]
            at += out.shape[0]


def fetch_kernel(*refs):
    count = len(refs) // 3
    copies = [pltpu.make_async_copy(*refs[i::count]) for i in range(count)]
    for copy in copies:
        copy.start()
    for copy in copies:
        copy.wait()


def fetch(*arrays):
    count = len(arrays)
    return pl.pallas_call(
        fetch_kernel,
        out_shape=[pltpu.VMEM(v.shape, v.dtype) for v in arrays],
        in_specs=[pl.BlockSpec(memory_space=pltpu.HBM)] * count,
        out_specs=[pl.BlockSpec(memory_space=pltpu.VMEM)] * count,
        scratch_shapes=[pltpu.SemaphoreType.DMA] * count,
        compiler_params=pltpu.CompilerParams(vmem_limit_bytes=1024 * 1024),
        cost_estimate=pl.CostEstimate(
            flops=0, transcendentals=0, bytes_accessed=sum(v.size * v.dtype.itemsize for v in arrays)
        ),
    )(*[pltpu.with_memory_space_constraint(v, pltpu.HBM) for v in arrays])


def expert(pieces, w_gate, w_up, w_down):
    count = len(pieces)
    total_rows = sum(p.shape[0] for p in pieces)
    inner, width = w_down.shape
    vmem = lambda n: [pl.BlockSpec(memory_space=pltpu.VMEM)] * n
    operands = [pltpu.with_memory_space_constraint(v, pltpu.VMEM) for v in (*pieces, w_gate, w_up, w_down)]
    return pl.pallas_call(
        functools.partial(expert_kernel, count),
        out_shape=[pltpu.VMEM(p.shape, p.dtype) for p in pieces],
        in_specs=vmem(count + 3),
        out_specs=vmem(count),
        scratch_shapes=[
            pltpu.VMEM((total_rows, width), jnp.bfloat16),
            pltpu.VMEM((total_rows, inner), jnp.bfloat16),
        ],
        compiler_params=pltpu.CompilerParams(vmem_limit_bytes=8 * 1024 * 1024),
        cost_estimate=pl.CostEstimate(
            flops=6 * total_rows * inner * width,
            transcendentals=total_rows * inner,
            bytes_accessed=6 * inner * width,
        ),
    )(*operands)


def total(*terms):
    value = terms[0].astype(jnp.float32)
    for term in terms[1:]:
        value = value + term.astype(jnp.float32)
    return value.astype(jnp.bfloat16)


together = lax.optimization_barrier


def shards(tokens, w_gate, w_up, w_down, route_ids, route_prob, slot_index):
    capacity = tokens.shape[0] // 2
    half = capacity // 2
    share = jnp.where(
        route_ids[:, 0] == 0, route_prob, jnp.where(route_ids[:, 1] == 0, 1.0 - route_prob, 0.0)
    )
    share = jnp.where(slot_index < capacity, share, 0.0)

    odd = lax.axis_index("z") % 2
    row = jnp.where(odd == 1, capacity - 1 - slot_index, slot_index)
    row = jnp.where(slot_index < capacity, row, -capacity)
    kept_row = row - odd * half
    sent_row = row - (1 - odd) * half
    lanes = jnp.arange(half, dtype=jnp.int32)[:, None]
    keep = (kept_row[None, :] == lanes).astype(jnp.bfloat16)
    send = (sent_row[None, :] == lanes).astype(jnp.bfloat16)
    sent = jnp.dot(send, tokens, preferred_element_type=jnp.float32).astype(jnp.bfloat16)
    arrived = swap_pair(sent)
    kept = jnp.dot(keep, tokens, preferred_element_type=jnp.float32).astype(jnp.bfloat16)
    arrived, kept = together((arrived, kept))
    own = arrived + kept

    up1, down1 = along_z(own, 1), along_z(own, -1)
    weights = fetch(w_gate, w_up, w_down)
    up1, down1, weights = together((up1, down1, weights))
    up2, down2 = along_z(up1, 1), along_z(down1, -1)
    y1 = along_y(jnp.concatenate([own, up1, down1]), 1)
    up2, down2 = together((up2, down2))
    up3, down3 = along_z(up2, 1), along_z(down2, -1)
    y2 = along_y(jnp.concatenate([up2, down2]), 1)
    up3, down3, y1 = together((up3, down3, y1))
    up4, y4 = along_z(up3, 1), diagonal(up3, 1, 1)
    y3 = along_y(jnp.concatenate([up3, down3]), 1)
    y2, *mine = together((y2, own, up1, down1, up2, down2, up3, down3))
    *mine, o1, o2 = expert([*mine, y1, y2], *weights)
    mine, up4, y3, y4 = together((mine, up4, y3, y4))
    m4, o3, o4 = expert([up4, y3, y4], *weights)

    f_down, g_down = along_z(m4, -1), diagonal(o4, -1, -1)
    b3 = along_y(o3, -1)
    f_down, g_down, b3 = together((f_down, g_down, b3))
    t_down = total(mine[5], b3[:half], f_down, g_down)
    t_up = total(mine[6], b3[half:])
    t_down, t_up = together((t_down, t_up))
    b2 = along_y(o2, -1)
    f_down, f_up = along_z(t_down, -1), along_z(t_up, 1)
    f_down, f_up, b2 = together((f_down, f_up, b2))
    t_down = total(mine[3], b2[:half], f_down)
    t_up = total(mine[4], b2[half:], f_up)
    t_down, t_up = together((t_down, t_up))
    b1 = along_y(o1, -1)
    f_down, f_up = along_z(t_down, -1), along_z(t_up, 1)
    f_down, f_up, b1 = together((f_down, f_up, b1))
    t_down = total(mine[1], b1[half : 2 * half], f_down)
    t_up = total(mine[2], b1[2 * half :], f_up)
    t_down, t_up = together((t_down, t_up))
    f_down, f_up = along_z(t_down, -1), along_z(t_up, 1)
    down_own = total(mine[0], b1[:half], f_down, f_up)

    down_other = swap_pair(down_own)
    placed = jnp.einsum("cr,cd->rd", keep, down_own, preferred_element_type=jnp.float32)
    placed = placed + jnp.einsum("cr,cd->rd", send, down_other, preferred_element_type=jnp.float32)
    return (share[:, None] * placed).astype(jnp.bfloat16)


def solution(mesh):
    fine = Mesh(mesh.devices.reshape(SIZES), AXES)
    every = ("y_hi", "x", "core", "y_lo", "z")
    group = ("y_lo", "z")
    return jax.shard_map(
        shards,
        mesh=fine,
        in_specs=(
            P(every, None),
            P(None, group),
            P(None, group),
            P(group, None),
            P(every, None),
            P(every),
            P(every),
        ),
        out_specs=P(every, None),
        check_vma=False,
    )
```

time: 115 us -> 95.2 us (0.83); the launches traced: 113 us -> 94.9 us
  matrix products: 21.5 us -> 2.16 us
  Pallas kernels: 0 us -> 9.12 us
  local copies, waits for them, and re-layouts: 9.2 us -> 0.43 us
  starting transfers between devices: 29.9 us -> 32.6 us
  other arithmetic: 2.91 us -> 1.41 us
    dot_general x4 -> x0, matrix products: 16.9 us -> none  [the longest x2 11 us: expert(): jnp.dot(hidden, w_down, preferred_element_type=jnp.float32)]
    pallas_call x0 -> x3, Pallas kernels: none -> 9.12 us  [the longest x2 5.34 us: expert(): pl.pallas_call(functools.partial(expert_kernel, count), out_shape=[pltpu....]
    ppermute x8 -> x6, waiting for transfers between devices: 8.8 us -> 1.39 us  [along_y(): return lax.ppermute(value, ('y_hi', 'core', 'y_lo'), pairs)]
    ppermute x16, waiting for transfers between devices: 29.9 us -> 37.3 us  [the longest x14 30.5 us: along_z(): return lax.ppermute(value, ('core', 'z'), pairs)]
    unnamed x24 -> x8, local copies, waits for them, and re-layouts: 4.23 us -> 0.43 us
    slice x6 -> x0, local copies, waits for them, and re-layouts: 3.36 us -> none  [the longest x3 3.33 us: piece(): return value[c * half:(c + count) * half]]
    ppermute x16, starting transfers between devices: 24.3 us -> 27.5 us  [the longest x14 23.4 us: along_z(): return lax.ppermute(value, ('core', 'z'), pairs)]
    concatenate x2 -> x0, local copies, waits for them, and re-layouts: 1.61 us -> none  [the longest x1 1.61 us: shards(): theirs = jnp.concatenate([y1, y2, y3, y4])]
  transfers between devices with their start and end apart: 26 -> 24, of which waited for: 17 -> 15; matrix products, arithmetic and copies ran while one was open for 12% -> 1% of each run, Pallas kernels for 0% -> 8%
where the time goes in v2:
time: 95.2 us; the launch traced here: 94.9 us
  waiting for transfers between devices  48.9 us (51%)
  starting transfers between devices  32.6 us (34%)
  Pallas kernels  9.12 us (10%)
  matrix products  2.16 us (2%)
  other arithmetic  1.41 us (1%)
    ppermute x14, waiting for transfers between devices, along_z(): return lax.ppermute(value, ('core', 'z'), pairs)  30.5 us
    ppermute x14, starting transfers between devices, along_z(): return lax.ppermute(value, ('core', 'z'), pairs)  23.4 us
    ppermute x2, waiting for transfers between devices, swap_pair(): return lax.ppermute(value, 'z', [(i, i ^ 1) for i in range(NZ)])  10.3 us
    ppermute x2, waiting for transfers between devices, diagonal(): return lax.ppermute(value, ('y_hi', 'core', 'y_lo', 'z'), pairs)  6.78 us
    pallas_call x2, Pallas kernels, expert(): pl.pallas_call(functools.partial(expert_kernel, count), out_shape=[pltpu....  5.34 us
    ppermute x2, starting transfers between devices, diagonal(): return lax.ppermute(value, ('y_hi', 'core', 'y_lo', 'z'), pairs)  4.09 us
    pallas_call x1, Pallas kernels, fetch(): pl.pallas_call(fetch_kernel, out_shape=[pltpu.VMEM(v.shape, v.dtype) for...  3.78 us
    ppermute x6, starting transfers between devices, along_y(): return lax.ppermute(value, ('y_hi', 'core', 'y_lo'), pairs)  3.04 us
  transfers between devices with their start and end apart: 24, of which 15 were waited for; matrix products, arithmetic and copies ran while one was open for 1% of the time, Pallas kernels for 8%

profile of v2, /device:TPU:26, one launch (start us, length us, event | category | flops | bytes accessed | tf_op | source)
XLA Modules:
  0.0 94.9 jit_solution(13988734286891328333)
XLA Ops:
  1.4 2.0 %collective-permute-start = (bf16[32,3072]{1,0:T(8,128)(2,1)S(1)}, bf16[32,3072]{1,0:T(8,128)(2,1)S(1)}, u32[]{:S(2)}, u32[]{:S(2)}) collective-permute-start(bf16[32,3072]{1,0:T(8,128)(2,1)S(1)} %convolution_convert_fusion.1), channel_id=1, source_target_pairs={{0,1},{1,0},{2,3},{3,2},{4,5},{5,4},{6,7},{7,6},{8,9},{9,8},{10,11... | collective-permute-start | bytes 589832 | tf_op jit(solution)/shard_map/ppermute | solution.py:37
  3.6 4.7 %collective-permute-done = bf16[32,3072]{1,0:T(8,128)(2,1)S(1)} collective-permute-done((bf16[32,3072]{1,0:T(8,128)(2,1)S(1)}, bf16[32,3072]{1,0:T(8,128)(2,1)S(1)}, u32[]{:S(2)}, u32[]{:S(2)}) %collective-permute-start) | collective-permute-done | bytes 196640 | tf_op jit(solution)/shard_map/ppermute | solution.py:37
  8.3 1.8 %collective-permute-start.1 = (bf16[32,3072]{1,0:T(8,128)(2,1)S(1)}, bf16[32,3072]{1,0:T(8,128)(2,1)S(1)}, u32[]{:S(2)}, u32[]{:S(2)}) collective-permute-start(bf16[32,3072]{1,0:T(8,128)(2,1)S(1)} %add.56.refs_0_), channel_id=1, source_target_pairs={{0,1},{1,2},{2,3},{3,4},{4,5},{5,6},{6,7},{7,0},{16,23},{17,16},{1... | collective-permute-start | bytes 589832 | tf_op jit(solution)/shard_map/ppermute | solution.py:23
  10.2 4.0 %collective-permute-start.2 = (bf16[32,3072]{1,0:T(8,128)(2,1)S(1)}, bf16[32,3072]{1,0:T(8,128)(2,1)S(1)}, u32[]{:S(2)}, u32[]{:S(2)}) collective-permute-start(bf16[32,3072]{1,0:T(8,128)(2,1)S(1)} %add.56.refs_0_), channel_id=1, source_target_pairs={{0,7},{1,0},{2,1},{3,2},{4,3},{5,4},{6,5},{7,6},{16,17},{17,18},{1... | collective-permute-start | bytes 589832 | tf_op jit(solution)/shard_map/ppermute | solution.py:23
  14.2 3.8 %shard_map.73 = (bf16[3072,512]{1,0:T(8,128)(2,1)S(1)}, bf16[3072,512]{1,0:T(8,128)(2,1)S(1)}, bf16[512,3072]{1,0:T(8,128)(2,1)S(1)}) custom-call(bf16[3072,512]{1,0:T(8,128)(2,1)} %refs_0_.1, bf16[3072,512]{1,0:T(8,128)(2,1)} %refs_1_.1, bf16[512,3072]{1,0:T(8,128)(2,1)} %refs_2_.1), custom_call_target="tpu_custom_call" | custom-call | bytes 9437184 | tf_op jit(solution)/shard_map/pallas_call | solution.py:87
  19.3 3.2 %collective-permute-start.4 = (bf16[32,3072]{1,0:T(8,128)(2,1)S(1)}, bf16[32,3072]{1,0:T(8,128)(2,1)S(1)}, u32[]{:S(2)}, u32[]{:S(2)}) collective-permute-start(bf16[32,3072]{1,0:T(8,128)(2,1)S(1)} %collective-permute-done.2.refs_2_), channel_id=1, source_target_pairs={{0,7},{1,0},{2,1},{3,2},{4,3},{5,4},{6,5},{7,6},{16,17},{17,18},{1... | collective-permute-start | bytes 589832 | tf_op jit(solution)/shard_map/ppermute | solution.py:23
  22.5 5.7 %collective-permute-done.3.refs_3_ = bf16[32,3072]{1,0:T(8,128)(2,1)S(1)} collective-permute-done((bf16[32,3072]{1,0:T(8,128)(2,1)S(1)}, bf16[32,3072]{1,0:T(8,128)(2,1)S(1)}, u32[]{:S(2)}, u32[]{:S(2)}) %collective-permute-start.3) | collective-permute-done | bytes 196640 | tf_op jit(solution)/shard_map/ppermute | solution.py:23
  28.2 3.2 %collective-permute-start.7 = (bf16[32,3072]{1,0:T(8,128)(2,1)S(1)}, bf16[32,3072]{1,0:T(8,128)(2,1)S(1)}, u32[]{:S(2)}, u32[]{:S(2)}) collective-permute-start(bf16[32,3072]{1,0:T(8,128)(2,1)S(1)} %collective-permute-done.4.refs_4_), channel_id=1, source_target_pairs={{0,7},{1,0},{2,1},{3,2},{4,3},{5,4},{6,5},{7,6},{16,17},{17,18},{1... | collective-permute-start | bytes 589832 | tf_op jit(solution)/shard_map/ppermute | solution.py:23
  32.2 4.1 %collective-permute-done.6.refs_5_ = bf16[32,3072]{1,0:T(8,128)(2,1)S(1)} collective-permute-done((bf16[32,3072]{1,0:T(8,128)(2,1)S(1)}, bf16[32,3072]{1,0:T(8,128)(2,1)S(1)}, u32[]{:S(2)}, u32[]{:S(2)}) %collective-permute-start.6) | collective-permute-done | bytes 196640 | tf_op jit(solution)/shard_map/ppermute | solution.py:23
  37.9 3.0 %collective-permute-start.11 = (bf16[32,3072]{1,0:T(8,128)(2,1)S(1)}, bf16[32,3072]{1,0:T(8,128)(2,1)S(1)}, u32[]{:S(2)}, u32[]{:S(2)}) collective-permute-start(bf16[32,3072]{1,0:T(8,128)(2,1)S(1)} %collective-permute-done.6.refs_5_), channel_id=1, source_target_pairs={{0,9},{1,10},{2,11},{3,12},{4,13},{5,14},{6,15},{7,8},{16,159},{17... | collective-permute-start | bytes 589832 | tf_op jit(solution)/shard_map/ppermute | solution.py:50
  41.0 3.8 %shard_map.74 = (bf16[32,3072]{1,0:T(8,128)(2,1)S(1)}, bf16[32,3072]{1,0:T(8,128)(2,1)S(1)}, bf16[32,3072]{1,0:T(8,128)(2,1)S(1)}, bf16[32,3072]{1,0:T(8,128)(2,...) custom-call(bf16[32,3072]{1,0:T(8,128)(2,1)S(1)} %add.56.refs_0_, ...), custom_call_target="tpu_custom_call" | custom-call | flops 3623878656 | bytes 9437184 | tf_op jit(solution)/shard_map/pallas_call | solution.py:106
  44.8 2.1 %collective-permute-done.11.refs_2_ = bf16[32,3072]{1,0:T(8,128)(2,1)S(1)} collective-permute-done((bf16[32,3072]{1,0:T(8,128)(2,1)S(1)}, bf16[32,3072]{1,0:T(8,128)(2,1)S(1)}, u32[]{:S(2)}, u32[]{:S(2)}) %collective-permute-start.11) | collective-permute-done | bytes 196640 | tf_op jit(solution)/shard_map/ppermute | solution.py:50
  48.9 2.8 %collective-permute-start.12 = (bf16[32,3072]{1,0:T(8,128)(2,1)S(1)}, bf16[32,3072]{1,0:T(8,128)(2,1)S(1)}, u32[]{:S(2)}, u32[]{:S(2)}) collective-permute-start(bf16[32,3072]{1,0:T(8,128)(2,1)S(1)} %get-tuple-element.101), channel_id=1, source_target_pairs={{0,7},{1,0},{2,1},{3,2},{4,3},{5,4},{6,5},{7,6},{16,17},{17,18},{1... | collective-permute-start | bytes 589832 | tf_op jit(solution)/shard_map/ppermute | solution.py:23
  52.8 2.1 %collective-permute-done.12 = bf16[32,3072]{1,0:T(8,128)(2,1)S(1)} collective-permute-done((bf16[32,3072]{1,0:T(8,128)(2,1)S(1)}, bf16[32,3072]{1,0:T(8,128)(2,1)S(1)}, u32[]{:S(2)}, u32[]{:S(2)}) %collective-permute-start.12) | collective-permute-done | bytes 196640 | tf_op jit(solution)/shard_map/ppermute | solution.py:23
  54.9 4.7 %collective-permute-done.13 = bf16[32,3072]{1,0:T(8,128)(2,1)S(1)} collective-permute-done((bf16[32,3072]{1,0:T(8,128)(2,1)S(1)}, bf16[32,3072]{1,0:T(8,128)(2,1)S(1)}, u32[]{:S(2)}, u32[]{:S(2)}) %collective-permute-start.13) | collective-permute-done | bytes 196640 | tf_op jit(solution)/shard_map/ppermute | solution.py:50
  59.8 2.8 %collective-permute-start.15 = (bf16[32,3072]{1,0:T(8,128)(2,1)S(1)}, bf16[32,3072]{1,0:T(8,128)(2,1)S(1)}, u32[]{:S(2)}, u32[]{:S(2)}) collective-permute-start(bf16[32,3072]{1,0:T(8,128)(2,1)S(1)} %get-tuple-element.108), channel_id=1, source_target_pairs={{0,7},{1,0},{2,1},{3,2},{4,3},{5,4},{6,5},{7,6},{16,17},{17,18},{1... | collective-permute-start | bytes 589832 | tf_op jit(solution)/shard_map/ppermute | solution.py:23
  63.8 1.9 %collective-permute-done.15 = bf16[32,3072]{1,0:T(8,128)(2,1)S(1)} collective-permute-done((bf16[32,3072]{1,0:T(8,128)(2,1)S(1)}, bf16[32,3072]{1,0:T(8,128)(2,1)S(1)}, u32[]{:S(2)}, u32[]{:S(2)}) %collective-permute-start.15) | collective-permute-done | bytes 196640 | tf_op jit(solution)/shard_map/ppermute | solution.py:23
  65.7 5.5 %collective-permute-done.16 = bf16[32,3072]{1,0:T(8,128)(2,1)S(1)} collective-permute-done((bf16[32,3072]{1,0:T(8,128)(2,1)S(1)}, bf16[32,3072]{1,0:T(8,128)(2,1)S(1)}, u32[]{:S(2)}, u32[]{:S(2)}) %collective-permute-start.16) | collective-permute-done | bytes 196640 | tf_op jit(solution)/shard_map/ppermute | solution.py:23
  71.5 2.0 %collective-permute-start.19 = (bf16[32,3072]{1,0:T(8,128)(2,1)S(1)}, bf16[32,3072]{1,0:T(8,128)(2,1)S(1)}, u32[]{:S(2)}, u32[]{:S(2)}) collective-permute-start(bf16[32,3072]{1,0:T(8,128)(2,1)S(1)} %get-tuple-element.116), channel_id=1, source_target_pairs={{0,1},{1,2},{2,3},{3,4},{4,5},{5,6},{6,7},{7,0},{16,23},{17,16},{1... | collective-permute-start | bytes 589832 | tf_op jit(solution)/shard_map/ppermute | solution.py:23
  73.7 4.4 %collective-permute-done.18 = bf16[32,3072]{1,0:T(8,128)(2,1)S(1)} collective-permute-done((bf16[32,3072]{1,0:T(8,128)(2,1)S(1)}, bf16[32,3072]{1,0:T(8,128)(2,1)S(1)}, u32[]{:S(2)}, u32[]{:S(2)}) %collective-permute-start.18) | collective-permute-done | bytes 196640 | tf_op jit(solution)/shard_map/ppermute | solution.py:23
  78.1 2.1 %collective-permute-done.19 = bf16[32,3072]{1,0:T(8,128)(2,1)S(1)} collective-permute-done((bf16[32,3072]{1,0:T(8,128)(2,1)S(1)}, bf16[32,3072]{1,0:T(8,128)(2,1)S(1)}, u32[]{:S(2)}, u32[]{:S(2)}) %collective-permute-start.19) | collective-permute-done | bytes 196640 | tf_op jit(solution)/shard_map/ppermute | solution.py:23
  80.4 3.2 %collective-permute-start.21 = (bf16[32,3072]{1,0:T(8,128)(2,1)S(1)}, bf16[32,3072]{1,0:T(8,128)(2,1)S(1)}, u32[]{:S(2)}, u32[]{:S(2)}) collective-permute-start(bf16[32,3072]{1,0:T(8,128)(2,1)S(1)} %get-tuple-element.123), channel_id=1, source_target_pairs={{0,7},{1,0},{2,1},{3,2},{4,3},{5,4},{6,5},{7,6},{16,17},{17,18},{1... | collective-permute-start | bytes 589832 | tf_op jit(solution)/shard_map/ppermute | solution.py:23
  83.6 3.6 %collective-permute-done.22 = bf16[32,3072]{1,0:T(8,128)(2,1)S(1)} collective-permute-done((bf16[32,3072]{1,0:T(8,128)(2,1)S(1)}, bf16[32,3072]{1,0:T(8,128)(2,1)S(1)}, u32[]{:S(2)}, u32[]{:S(2)}) %collective-permute-start.22) | collective-permute-done | bytes 196640 | tf_op jit(solution)/shard_map/ppermute | solution.py:23
  87.5 5.6 %collective-permute-done.23 = bf16[32,3072]{1,0:T(8,128)(2,1)S(1)} collective-permute-done((bf16[32,3072]{1,0:T(8,128)(2,1)S(1)}, bf16[32,3072]{1,0:T(8,128)(2,1)S(1)}, u32[]{:S(2)}, u32[]{:S(2)}) %collective-permute-start.23) | collective-permute-done | bytes 196640 | tf_op jit(solution)/shard_map/ppermute | solution.py:37
  (49 shorter events, 12.2 us)
Async XLA Ops:
  1.4 6.9 %collective-permute-start = (bf16[32,3072]{1,0:T(8,128)(2,1)S(1)}, bf16[32,3072]{1,0:T(8,128)(2,1)S(1)}, u32[]{:S(2)}, u32[]{:S(2)}) collective-permute-start(bf16[32,3072]{1,0:T(8,128)(2,1)S(1)} %convolution_convert_fusion.1), channel_id=1, source_target_pairs={{0,1},{1,0},{2,3},{3,2},{4,5},{5,4},{6,7},{7,6},{8,9},{9,8},{10,11... | collective-permute-start | bytes 589832 | tf_op jit(solution)/shard_map/ppermute | solution.py:37
  8.3 10.6 %collective-permute-start.1 = (bf16[32,3072]{1,0:T(8,128)(2,1)S(1)}, bf16[32,3072]{1,0:T(8,128)(2,1)S(1)}, u32[]{:S(2)}, u32[]{:S(2)}) collective-permute-start(bf16[32,3072]{1,0:T(8,128)(2,1)S(1)} %add.56.refs_0_), channel_id=1, source_target_pairs={{0,1},{1,2},{2,3},{3,4},{4,5},{5,6},{6,7},{7,0},{16,23},{17,16},{1... | collective-permute-start | bytes 589832 | tf_op jit(solution)/shard_map/ppermute | solution.py:23
  10.2 8.8 %collective-permute-start.2 = (bf16[32,3072]{1,0:T(8,128)(2,1)S(1)}, bf16[32,3072]{1,0:T(8,128)(2,1)S(1)}, u32[]{:S(2)}, u32[]{:S(2)}) collective-permute-start(bf16[32,3072]{1,0:T(8,128)(2,1)S(1)} %add.56.refs_0_), channel_id=1, source_target_pairs={{0,7},{1,0},{2,1},{3,2},{4,3},{5,4},{6,5},{7,6},{16,17},{17,18},{1... | collective-permute-start | bytes 589832 | tf_op jit(solution)/shard_map/ppermute | solution.py:23
  19.0 17.4 %collective-permute-start.8 = (bf16[96,3072]{1,0:T(8,128)(2,1)S(1)}, bf16[96,3072]{1,0:T(8,128)(2,1)S(1)}, u32[]{:S(2)}, u32[]{:S(2)}) collective-permute-start(bf16[96,3072]{1,0:T(8,128)(2,1)S(1)} %pad_maximum_fusion), channel_id=1, source_target_pairs={{0,8},{16,152},{8,128},{24,16},{128,136},{144,24},{136,0},{152,144... | collective-permute-start | bytes 1769480 | tf_op jit(solution)/shard_map/ppermute | solution.py:33
  19.3 9.0 %collective-permute-start.3 = (bf16[32,3072]{1,0:T(8,128)(2,1)S(1)}, bf16[32,3072]{1,0:T(8,128)(2,1)S(1)}, u32[]{:S(2)}, u32[]{:S(2)}) collective-permute-start(bf16[32,3072]{1,0:T(8,128)(2,1)S(1)} %collective-permute-done.1.refs_1_), channel_id=1, source_target_pairs={{0,1},{1,2},{2,3},{3,4},{4,5},{5,6},{6,7},{7,0},{16,23},{17,16},{1... | collective-permute-start | bytes 589832 | tf_op jit(solution)/shard_map/ppermute | solution.py:23
  19.3 9.0 %collective-permute-start.4 = (bf16[32,3072]{1,0:T(8,128)(2,1)S(1)}, bf16[32,3072]{1,0:T(8,128)(2,1)S(1)}, u32[]{:S(2)}, u32[]{:S(2)}) collective-permute-start(bf16[32,3072]{1,0:T(8,128)(2,1)S(1)} %collective-permute-done.2.refs_2_), channel_id=1, source_target_pairs={{0,7},{1,0},{2,1},{3,2},{4,3},{5,4},{6,5},{7,6},{16,17},{17,18},{1... | collective-permute-start | bytes 589832 | tf_op jit(solution)/shard_map/ppermute | solution.py:23
  28.2 8.1 %collective-permute-start.6 = (bf16[32,3072]{1,0:T(8,128)(2,1)S(1)}, bf16[32,3072]{1,0:T(8,128)(2,1)S(1)}, u32[]{:S(2)}, u32[]{:S(2)}) collective-permute-start(bf16[32,3072]{1,0:T(8,128)(2,1)S(1)} %collective-permute-done.3.refs_3_), channel_id=1, source_target_pairs={{0,1},{1,2},{2,3},{3,4},{4,5},{5,6},{6,7},{7,0},{16,23},{17,16},{1... | collective-permute-start | bytes 589832 | tf_op jit(solution)/shard_map/ppermute | solution.py:23
  28.2 8.1 %collective-permute-start.7 = (bf16[32,3072]{1,0:T(8,128)(2,1)S(1)}, bf16[32,3072]{1,0:T(8,128)(2,1)S(1)}, u32[]{:S(2)}, u32[]{:S(2)}) collective-permute-start(bf16[32,3072]{1,0:T(8,128)(2,1)S(1)} %collective-permute-done.4.refs_4_), channel_id=1, source_target_pairs={{0,7},{1,0},{2,1},{3,2},{4,3},{5,4},{6,5},{7,6},{16,17},{17,18},{1... | collective-permute-start | bytes 589832 | tf_op jit(solution)/shard_map/ppermute | solution.py:23
  31.5 9.5 %collective-permute-start.5 = (bf16[64,3072]{1,0:T(8,128)(2,1)S(1)}, bf16[64,3072]{1,0:T(8,128)(2,1)S(1)}, u32[]{:S(2)}, u32[]{:S(2)}) collective-permute-start(bf16[64,3072]{1,0:T(8,128)(2,1)S(1)} %pad_maximum_fusion.1), channel_id=1, source_target_pairs={{0,8},{16,152},{8,128},{24,16},{128,136},{144,24},{136,0},{152,144... | collective-permute-start | bytes 1179656 | tf_op jit(solution)/shard_map/ppermute | solution.py:33
  36.4 10.5 %collective-permute-start.10 = (bf16[64,3072]{1,0:T(8,128)(2,1)S(1)}, bf16[64,3072]{1,0:T(8,128)(2,1)S(1)}, u32[]{:S(2)}, u32[]{:S(2)}) collective-permute-start(bf16[64,3072]{1,0:T(8,128)(2,1)S(1)} %pad_maximum_fusion.2), channel_id=1, source_target_pairs={{0,8},{16,152},{8,128},{24,16},{128,136},{144,24},{136,0},{152,144... | collective-permute-start | bytes 1179656 | tf_op jit(solution)/shard_map/ppermute | solution.py:33
  37.9 6.9 %collective-permute-start.9 = (bf16[32,3072]{1,0:T(8,128)(2,1)S(1)}, bf16[32,3072]{1,0:T(8,128)(2,1)S(1)}, u32[]{:S(2)}, u32[]{:S(2)}) collective-permute-start(bf16[32,3072]{1,0:T(8,128)(2,1)S(1)} %collective-permute-done.6.refs_5_), channel_id=1, source_target_pairs={{0,1},{1,2},{2,3},{3,4},{4,5},{5,6},{6,7},{7,0},{16,23},{17,16},{1... | collective-permute-start | bytes 589832 | tf_op jit(solution)/shard_map/ppermute | solution.py:23
  37.9 9.0 %collective-permute-start.11 = (bf16[32,3072]{1,0:T(8,128)(2,1)S(1)}, bf16[32,3072]{1,0:T(8,128)(2,1)S(1)}, u32[]{:S(2)}, u32[]{:S(2)}) collective-permute-start(bf16[32,3072]{1,0:T(8,128)(2,1)S(1)} %collective-permute-done.6.refs_5_), channel_id=1, source_target_pairs={{0,9},{1,10},{2,11},{3,12},{4,13},{5,14},{6,15},{7,8},{16,159},{17... | collective-permute-start | bytes 589832 | tf_op jit(solution)/shard_map/ppermute | solution.py:50
  48.4 11.2 %collective-permute-start.14 = (bf16[64,3072]{1,0:T(8,128)(2,1)S(1)}, bf16[64,3072]{1,0:T(8,128)(2,1)S(1)}, u32[]{:S(2)}, u32[]{:S(2)}) collective-permute-start(bf16[64,3072]{1,0:T(8,128)(2,1)S(1)} %get-tuple-element.103), channel_id=1, source_target_pairs={{0,136},{16,24},{8,0},{24,144},{128,8},{144,152},{136,128},{152,16... | collective-permute-start | bytes 1179656 | tf_op jit(solution)/shard_map/ppermute | solution.py:33
  48.9 6.0 %collective-permute-start.12 = (bf16[32,3072]{1,0:T(8,128)(2,1)S(1)}, bf16[32,3072]{1,0:T(8,128)(2,1)S(1)}, u32[]{:S(2)}, u32[]{:S(2)}) collective-permute-start(bf16[32,3072]{1,0:T(8,128)(2,1)S(1)} %get-tuple-element.101), channel_id=1, source_target_pairs={{0,7},{1,0},{2,1},{3,2},{4,3},{5,4},{6,5},{7,6},{16,17},{17,18},{1... | collective-permute-start | bytes 589832 | tf_op jit(solution)/shard_map/ppermute | solution.py:23
  51.7 7.9 %collective-permute-start.13 = (bf16[32,3072]{1,0:T(8,128)(2,1)S(1)}, bf16[32,3072]{1,0:T(8,128)(2,1)S(1)}, u32[]{:S(2)}, u32[]{:S(2)}) collective-permute-start(bf16[32,3072]{1,0:T(8,128)(2,1)S(1)} %get-tuple-element.102), channel_id=1, source_target_pairs={{0,143},{1,136},{2,137},{3,138},{4,139},{5,140},{6,141},{7,142},{1... | collective-permute-start | bytes 589832 | tf_op jit(solution)/shard_map/ppermute | solution.py:50
  52.8 11.1 %collective-permute-start.17 = (bf16[64,3072]{1,0:T(8,128)(2,1)S(1)}, bf16[64,3072]{1,0:T(8,128)(2,1)S(1)}, u32[]{:S(2)}, u32[]{:S(2)}) collective-permute-start(bf16[64,3072]{1,0:T(8,128)(2,1)S(1)} %get-tuple-element.110), channel_id=1, source_target_pairs={{0,136},{16,24},{8,0},{24,144},{128,8},{144,152},{136,128},{152,16... | collective-permute-start | bytes 1179656 | tf_op jit(solution)/shard_map/ppermute | solution.py:33
  59.8 6.0 %collective-permute-start.15 = (bf16[32,3072]{1,0:T(8,128)(2,1)S(1)}, bf16[32,3072]{1,0:T(8,128)(2,1)S(1)}, u32[]{:S(2)}, u32[]{:S(2)}) collective-permute-start(bf16[32,3072]{1,0:T(8,128)(2,1)S(1)} %get-tuple-element.108), channel_id=1, source_target_pairs={{0,7},{1,0},{2,1},{3,2},{4,3},{5,4},{6,5},{7,6},{16,17},{17,18},{1... | collective-permute-start | bytes 589832 | tf_op jit(solution)/shard_map/ppermute | solution.py:23
  62.6 8.7 %collective-permute-start.16 = (bf16[32,3072]{1,0:T(8,128)(2,1)S(1)}, bf16[32,3072]{1,0:T(8,128)(2,1)S(1)}, u32[]{:S(2)}, u32[]{:S(2)}) collective-permute-start(bf16[32,3072]{1,0:T(8,128)(2,1)S(1)} %get-tuple-element.109), channel_id=1, source_target_pairs={{0,1},{1,2},{2,3},{3,4},{4,5},{5,6},{6,7},{7,0},{16,23},{17,16},{1... | collective-permute-start | bytes 589832 | tf_op jit(solution)/shard_map/ppermute | solution.py:23
  62.6 11.1 %collective-permute-start.20 = (bf16[96,3072]{1,0:T(8,128)(2,1)S(1)}, bf16[96,3072]{1,0:T(8,128)(2,1)S(1)}, u32[]{:S(2)}, u32[]{:S(2)}) collective-permute-start(bf16[96,3072]{1,0:T(8,128)(2,1)S(1)} %get-tuple-element.117), channel_id=1, source_target_pairs={{0,136},{16,24},{8,0},{24,144},{128,8},{144,152},{136,128},{152,16... | collective-permute-start | bytes 1769480 | tf_op jit(solution)/shard_map/ppermute | solution.py:33
  71.4 6.7 %collective-permute-start.18 = (bf16[32,3072]{1,0:T(8,128)(2,1)S(1)}, bf16[32,3072]{1,0:T(8,128)(2,1)S(1)}, u32[]{:S(2)}, u32[]{:S(2)}) collective-permute-start(bf16[32,3072]{1,0:T(8,128)(2,1)S(1)} %get-tuple-element.115), channel_id=1, source_target_pairs={{0,7},{1,0},{2,1},{3,2},{4,3},{5,4},{6,5},{7,6},{16,17},{17,18},{1... | collective-permute-start | bytes 589832 | tf_op jit(solution)/shard_map/ppermute | solution.py:23
  71.5 8.7 %collective-permute-start.19 = (bf16[32,3072]{1,0:T(8,128)(2,1)S(1)}, bf16[32,3072]{1,0:T(8,128)(2,1)S(1)}, u32[]{:S(2)}, u32[]{:S(2)}) collective-permute-start(bf16[32,3072]{1,0:T(8,128)(2,1)S(1)} %get-tuple-element.116), channel_id=1, source_target_pairs={{0,1},{1,2},{2,3},{3,4},{4,5},{5,6},{6,7},{7,0},{16,23},{17,16},{1... | collective-permute-start | bytes 589832 | tf_op jit(solution)/shard_map/ppermute | solution.py:23
  80.3 7.0 %collective-permute-start.22 = (bf16[32,3072]{1,0:T(8,128)(2,1)S(1)}, bf16[32,3072]{1,0:T(8,128)(2,1)S(1)}, u32[]{:S(2)}, u32[]{:S(2)}) collective-permute-start(bf16[32,3072]{1,0:T(8,128)(2,1)S(1)} %get-tuple-element.124), channel_id=1, source_target_pairs={{0,1},{1,2},{2,3},{3,4},{4,5},{5,6},{6,7},{7,0},{16,23},{17,16},{1... | collective-permute-start | bytes 589832 | tf_op jit(solution)/shard_map/ppermute | solution.py:23
  80.4 6.9 %collective-permute-start.21 = (bf16[32,3072]{1,0:T(8,128)(2,1)S(1)}, bf16[32,3072]{1,0:T(8,128)(2,1)S(1)}, u32[]{:S(2)}, u32[]{:S(2)}) collective-permute-start(bf16[32,3072]{1,0:T(8,128)(2,1)S(1)} %get-tuple-element.123), channel_id=1, source_target_pairs={{0,7},{1,0},{2,1},{3,2},{4,3},{5,4},{6,5},{7,6},{16,17},{17,18},{1... | collective-permute-start | bytes 589832 | tf_op jit(solution)/shard_map/ppermute | solution.py:23
  87.4 5.8 %collective-permute-start.23 = (bf16[32,3072]{1,0:T(8,128)(2,1)S(1)}, bf16[32,3072]{1,0:T(8,128)(2,1)S(1)}, u32[]{:S(2)}, u32[]{:S(2)}) collective-permute-start(bf16[32,3072]{1,0:T(8,128)(2,1)S(1)} %add_convert_fusion), channel_id=1, source_target_pairs={{0,1},{1,0},{2,3},{3,2},{4,5},{5,4},{6,7},{7,6},{8,9},{9,8},{10,11... | collective-permute-start | bytes 589832 | tf_op jit(solution)/shard_map/ppermute | solution.py:37
  (4 other events, 49.4 us)

commit v3 on v2

--- a/solution.py
+++ b/solution.py
@@ -14,6 +14,10 @@
 
 
 def along_z(value, step):
+    return lax.ppermute(value, "z", [(i, (i + step) % NZ) for i in range(NZ)])
+
+
+def along_z_by_core(value, step):
     def index(core, z):
         return core * NZ + z
 
@@ -153,27 +157,27 @@
     arrived, kept = together((arrived, kept))
     own = arrived + kept
 
+    first = lax.axis_index("core") == 0
     up1, down1 = along_z(own, 1), along_z(own, -1)
     weights = fetch(w_gate, w_up, w_down)
-    up1, down1, weights = together((up1, down1, weights))
+    down1, weights = together((down1, weights))
     up2, down2 = along_z(up1, 1), along_z(down1, -1)
     y1 = along_y(jnp.concatenate([own, up1, down1]), 1)
-    up2, down2 = together((up2, down2))
     up3, down3 = along_z(up2, 1), along_z(down2, -1)
     y2 = along_y(jnp.concatenate([up2, down2]), 1)
-    up3, down3, y1 = together((up3, down3, y1))
-    up4, y4 = along_z(up3, 1), diagonal(up3, 1, 1)
+    last = jnp.where(first, up3, down3)
+    far, y4 = along_z_by_core(last, 1), diagonal(last, 1, 1)
     y3 = along_y(jnp.concatenate([up3, down3]), 1)
-    y2, *mine = together((y2, own, up1, down1, up2, down2, up3, down3))
+    y1, y2, *mine = together((y1, y2, own, up1, down1, up2, down2, up3, down3))
     *mine, o1, o2 = expert([*mine, y1, y2], *weights)
-    mine, up4, y3, y4 = together((mine, up4, y3, y4))
-    m4, o3, o4 = expert([up4, y3, y4], *weights)
-
-    f_down, g_down = along_z(m4, -1), diagonal(o4, -1, -1)
+    mine, far, y3, y4 = together((mine, far, y3, y4))
+    m4, o3, o4 = expert([far, y3, y4], *weights)
+
+    f, g = along_z_by_core(m4, -1), diagonal(o4, -1, -1)
     b3 = along_y(o3, -1)
-    f_down, g_down, b3 = together((f_down, g_down, b3))
-    t_down = total(mine[5], b3[:half], f_down, g_down)
-    t_up = total(mine[6], b3[half:])
+    f, g, b3 = together((f, g, b3))
+    t_down = total(mine[5], b3[:half], jnp.where(first, f, 0), jnp.where(first, g, 0))
+    t_up = total(mine[6], b3[half:], jnp.where(first, 0, f), jnp.where(first, 0, g))
     t_down, t_up = together((t_down, t_up))
     b2 = along_y(o2, -1)
     f_down, f_up = along_z(t_down, -1), along_z(t_up, 1)
@@ -192,6 +196,7 @@
 
     down_other = swap_pair(down_own)
     placed = jnp.einsum("cr,cd->rd", keep, down_own, preferred_element_type=jnp.float32)
+    down_other, placed = together((down_other, placed))
     placed = placed + jnp.einsum("cr,cd->rd", send, down_other, preferred_element_type=jnp.float32)
     return (share[:, None] * placed).astype(jnp.bfloat16)
 

time: 95.2 us -> 92.1 us (0.967); the launches traced: 94.9 us -> 90.4 us
  starting transfers between devices: 32.6 us -> 25.6 us
  waiting for transfers between devices: 48.9 us -> 51.2 us
  other arithmetic: 1.41 us -> 2.64 us
    ppermute x14, starting transfers between devices: 23.4 us -> 19.3 us  [the longest x12 19.1 us: along_z(): return lax.ppermute(value, 'z', [(i, (i + step) % NZ) for i in range(NZ)])]
    ppermute x2, starting transfers between devices: 4.09 us -> 1.08 us  [diagonal(): return lax.ppermute(value, ('y_hi', 'core', 'y_lo', 'z'), pairs)]
    ppermute x2, waiting for transfers between devices: 6.78 us -> 9.33 us  [diagonal(): return lax.ppermute(value, ('y_hi', 'core', 'y_lo', 'z'), pairs)]
    ppermute x6, waiting for transfers between devices: 1.39 us -> 3.55 us  [along_y(): return lax.ppermute(value, ('y_hi', 'core', 'y_lo'), pairs)]
    ppermute x14, waiting for transfers between devices: 30.5 us -> 28.9 us  [the longest x12 22.9 us: along_z(): return lax.ppermute(value, 'z', [(i, (i + step) % NZ) for i in range(NZ)])]
    convert_element_type x0 -> x1, other arithmetic: none -> 1.11 us  [shards(): return (share[:, None] * placed).astype(jnp.bfloat16)]
  transfers between devices with their start and end apart: 24 -> 24, of which waited for: 15 -> 18; matrix products, arithmetic and copies ran while one was open for 1% -> 1% of each run, Pallas kernels for 8% -> 8%
where the time goes in v3:
time: 92.1 us; the launch traced here: 90.4 us
  waiting for transfers between devices  51.2 us (56%)
  starting transfers between devices  25.6 us (28%)
  Pallas kernels  9.13 us (10%)
  other arithmetic  2.64 us (3%)
  matrix products  1.27 us (1%)
    ppermute x12, waiting for transfers between devices, along_z(): return lax.ppermute(value, 'z', [(i, (i + step) % NZ) for i in range(NZ)])  22.9 us
    ppermute x12, starting transfers between devices, along_z(): return lax.ppermute(value, 'z', [(i, (i + step) % NZ) for i in range(NZ)])  19.1 us
    ppermute x2, waiting for transfers between devices, swap_pair(): return lax.ppermute(value, 'z', [(i, i ^ 1) for i in range(NZ)])  9.39 us
    ppermute x2, waiting for transfers between devices, diagonal(): return lax.ppermute(value, ('y_hi', 'core', 'y_lo', 'z'), pairs)  9.33 us
    ppermute x2, waiting for transfers between devices, along_z_by_core(): return lax.ppermute(value, ('core', 'z'), pairs)  6.03 us
    pallas_call x2, Pallas kernels, expert(): pl.pallas_call(functools.partial(expert_kernel, count), out_shape=[pltpu....  5.35 us
    pallas_call x1, Pallas kernels, fetch(): pl.pallas_call(fetch_kernel, out_shape=[pltpu.VMEM(v.shape, v.dtype) for...  3.78 us
    ppermute x6, waiting for transfers between devices, along_y(): return lax.ppermute(value, ('y_hi', 'core', 'y_lo'), pairs)  3.55 us
  transfers between devices with their start and end apart: 24, of which 18 were waited for; matrix products, arithmetic and copies ran while one was open for 1% of the time, Pallas kernels for 8%

profile of v3, /device:TPU:26, one launch (start us, length us, event | category | flops | bytes accessed | tf_op | source)
XLA Modules:
  0.0 90.4 jit_solution(12339155485292156345)
XLA Ops:
  1.4 2.0 %collective-permute-start = (bf16[32,3072]{1,0:T(8,128)(2,1)S(1)}, bf16[32,3072]{1,0:T(8,128)(2,1)S(1)}, u32[]{:S(2)}, u32[]{:S(2)}) collective-permute-start(bf16[32,3072]{1,0:T(8,128)(2,1)S(1)} %convolution_convert_fusion.1), channel_id=1, source_target_pairs={{0,1},{1,0},{2,3},{3,2},{4,5},{5,4},{6,7},{7,6},{8,9},{9,8},{10,11... | collective-permute-start | bytes 589832 | tf_op jit(solution)/shard_map/ppermute | solution.py:41
  3.6 4.7 %collective-permute-done = bf16[32,3072]{1,0:T(8,128)(2,1)S(1)} collective-permute-done((bf16[32,3072]{1,0:T(8,128)(2,1)S(1)}, bf16[32,3072]{1,0:T(8,128)(2,1)S(1)}, u32[]{:S(2)}, u32[]{:S(2)}) %collective-permute-start) | collective-permute-done | bytes 196640 | tf_op jit(solution)/shard_map/ppermute | solution.py:41
  8.3 5.8 %collective-permute-start.2 = (bf16[32,3072]{1,0:T(8,128)(2,1)S(1)}, bf16[32,3072]{1,0:T(8,128)(2,1)S(1)}, u32[]{:S(2)}, u32[]{:S(2)}) collective-permute-start(bf16[32,3072]{1,0:T(8,128)(2,1)S(1)} %add.62.refs_0_), channel_id=1, source_target_pairs={{0,7},{1,0},{2,1},{3,2},{4,3},{5,4},{6,5},{7,6},{8,15},{9,8},{10,9... | collective-permute-start | bytes 589832 | tf_op jit(solution)/shard_map/ppermute | solution.py:17
  14.1 3.8 %shard_map.73 = (bf16[3072,512]{1,0:T(8,128)(2,1)S(1)}, bf16[3072,512]{1,0:T(8,128)(2,1)S(1)}, bf16[512,3072]{1,0:T(8,128)(2,1)S(1)}) custom-call(bf16[3072,512]{1,0:T(8,128)(2,1)} %refs_0_.1, bf16[3072,512]{1,0:T(8,128)(2,1)} %refs_1_.1, bf16[512,3072]{1,0:T(8,128)(2,1)} %refs_2_.1), custom_call_target="tpu_custom_call" | custom-call | bytes 9437184 | tf_op jit(solution)/shard_map/pallas_call | solution.py:91
  17.9 3.3 %collective-permute-start.5 = (bf16[32,3072]{1,0:T(8,128)(2,1)S(1)}, bf16[32,3072]{1,0:T(8,128)(2,1)S(1)}, u32[]{:S(2)}, u32[]{:S(2)}) collective-permute-start(bf16[32,3072]{1,0:T(8,128)(2,1)S(1)} %collective-permute-done.2.refs_2_), channel_id=1, source_target_pairs={{0,7},{1,0},{2,1},{3,2},{4,3},{5,4},{6,5},{7,6},{8,15},{9,8},{10,9... | collective-permute-start | bytes 589832 | tf_op jit(solution)/shard_map/ppermute | solution.py:17
  21.6 2.8 %collective-permute-done.5.refs_4_ = bf16[32,3072]{1,0:T(8,128)(2,1)S(1)} collective-permute-done((bf16[32,3072]{1,0:T(8,128)(2,1)S(1)}, bf16[32,3072]{1,0:T(8,128)(2,1)S(1)}, u32[]{:S(2)}, u32[]{:S(2)}) %collective-permute-start.5) | collective-permute-done | bytes 196640 | tf_op jit(solution)/shard_map/ppermute | solution.py:17
  24.4 3.7 %collective-permute-start.8 = (bf16[32,3072]{1,0:T(8,128)(2,1)S(1)}, bf16[32,3072]{1,0:T(8,128)(2,1)S(1)}, u32[]{:S(2)}, u32[]{:S(2)}) collective-permute-start(bf16[32,3072]{1,0:T(8,128)(2,1)S(1)} %collective-permute-done.5.refs_4_), channel_id=1, source_target_pairs={{0,7},{1,0},{2,1},{3,2},{4,3},{5,4},{6,5},{7,6},{8,15},{9,8},{10,9... | collective-permute-start | bytes 589832 | tf_op jit(solution)/shard_map/ppermute | solution.py:17
  28.4 2.9 %collective-permute-done.8.refs_6_ = bf16[32,3072]{1,0:T(8,128)(2,1)S(1)} collective-permute-done((bf16[32,3072]{1,0:T(8,128)(2,1)S(1)}, bf16[32,3072]{1,0:T(8,128)(2,1)S(1)}, u32[]{:S(2)}, u32[]{:S(2)}) %collective-permute-start.8) | collective-permute-done | bytes 196640 | tf_op jit(solution)/shard_map/ppermute | solution.py:17
  31.3 3.7 %collective-permute-done.7.refs_5_ = bf16[32,3072]{1,0:T(8,128)(2,1)S(1)} collective-permute-done((bf16[32,3072]{1,0:T(8,128)(2,1)S(1)}, bf16[32,3072]{1,0:T(8,128)(2,1)S(1)}, u32[]{:S(2)}, u32[]{:S(2)}) %collective-permute-start.7) | collective-permute-done | bytes 196640 | tf_op jit(solution)/shard_map/ppermute | solution.py:17
  36.0 3.8 %shard_map.74 = (bf16[32,3072]{1,0:T(8,128)(2,1)S(1)}, bf16[32,3072]{1,0:T(8,128)(2,1)S(1)}, bf16[32,3072]{1,0:T(8,128)(2,1)S(1)}, bf16[32,3072]{1,0:T(8,128)(2,...) custom-call(bf16[32,3072]{1,0:T(8,128)(2,1)S(1)} %add.62.refs_0_, ...), custom_call_target="tpu_custom_call" | custom-call | flops 3623878656 | bytes 9437184 | tf_op jit(solution)/shard_map/pallas_call | solution.py:110
  39.8 3.5 %collective-permute-done.11.refs_2_ = bf16[32,3072]{1,0:T(8,128)(2,1)S(1)} collective-permute-done((bf16[32,3072]{1,0:T(8,128)(2,1)S(1)}, bf16[32,3072]{1,0:T(8,128)(2,1)S(1)}, u32[]{:S(2)}, u32[]{:S(2)}) %collective-permute-start.11) | collective-permute-done | bytes 196640 | tf_op jit(solution)/shard_map/ppermute | solution.py:54
  43.3 2.1 %collective-permute-done.9.refs_0_ = bf16[32,3072]{1,0:T(8,128)(2,1)S(1)} collective-permute-done((bf16[32,3072]{1,0:T(8,128)(2,1)S(1)}, bf16[32,3072]{1,0:T(8,128)(2,1)S(1)}, u32[]{:S(2)}, u32[]{:S(2)}) %collective-permute-start.9) | collective-permute-done | bytes 196640 | tf_op jit(solution)/shard_map/ppermute | solution.py:27
  45.4 1.5 %shard_map.75 = (bf16[32,3072]{1,0:T(8,128)(2,1)S(1)}, bf16[64,3072]{1,0:T(8,128)(2,1)S(1)}, bf16[32,3072]{1,0:T(8,128)(2,1)S(1)}) custom-call(bf16[32,3072]{1,0:T(8,128)(2,1)S(1)} %collective-permute-done.9.refs_0_, bf16[64,3072]{1,0:T(8,128)(2,1)S(1)} %collective-permute-done.10.refs_1_, bf16[32,3072]{1,0:T(8,128)(2,1)S(1)} %collective-permute-done.11.refs_2_, ...), custom_call_target="tpu_custom_call" | custom-call | flops 1207959552 | bytes 9437184 | tf_op jit(solution)/shard_map/pallas_call | solution.py:110
  49.6 3.9 %collective-permute-done.12 = bf16[32,3072]{1,0:T(8,128)(2,1)S(1)} collective-permute-done((bf16[32,3072]{1,0:T(8,128)(2,1)S(1)}, bf16[32,3072]{1,0:T(8,128)(2,1)S(1)}, u32[]{:S(2)}, u32[]{:S(2)}) %collective-permute-start.12) | collective-permute-done | bytes 196640 | tf_op jit(solution)/shard_map/ppermute | solution.py:27
  53.5 5.9 %collective-permute-done.13 = bf16[32,3072]{1,0:T(8,128)(2,1)S(1)} collective-permute-done((bf16[32,3072]{1,0:T(8,128)(2,1)S(1)}, bf16[32,3072]{1,0:T(8,128)(2,1)S(1)}, u32[]{:S(2)}, u32[]{:S(2)}) %collective-permute-start.13) | collective-permute-done | bytes 196640 | tf_op jit(solution)/shard_map/ppermute | solution.py:54
  59.7 2.0 %collective-permute-start.16 = (bf16[32,3072]{1,0:T(8,128)(2,1)S(1)}, bf16[32,3072]{1,0:T(8,128)(2,1)S(1)}, u32[]{:S(2)}, u32[]{:S(2)}) collective-permute-start(bf16[32,3072]{1,0:T(8,128)(2,1)S(1)} %get-tuple-element.101), channel_id=1, source_target_pairs={{0,1},{1,2},{2,3},{3,4},{4,5},{5,6},{6,7},{7,0},{8,9},{9,10},{10,1... | collective-permute-start | bytes 589832 | tf_op jit(solution)/shard_map/ppermute | solution.py:17
  62.3 4.3 %collective-permute-done.15 = bf16[32,3072]{1,0:T(8,128)(2,1)S(1)} collective-permute-done((bf16[32,3072]{1,0:T(8,128)(2,1)S(1)}, bf16[32,3072]{1,0:T(8,128)(2,1)S(1)}, u32[]{:S(2)}, u32[]{:S(2)}) %collective-permute-start.15) | collective-permute-done | bytes 196640 | tf_op jit(solution)/shard_map/ppermute | solution.py:17
  68.3 1.8 %collective-permute-start.19 = (bf16[32,3072]{1,0:T(8,128)(2,1)S(1)}, bf16[32,3072]{1,0:T(8,128)(2,1)S(1)}, u32[]{:S(2)}, u32[]{:S(2)}) collective-permute-start(bf16[32,3072]{1,0:T(8,128)(2,1)S(1)} %get-tuple-element.108), channel_id=1, source_target_pairs={{0,1},{1,2},{2,3},{3,4},{4,5},{5,6},{6,7},{7,0},{8,9},{9,10},{10,1... | collective-permute-start | bytes 589832 | tf_op jit(solution)/shard_map/ppermute | solution.py:17
  70.2 2.7 %collective-permute-done.20 = bf16[96,3072]{1,0:T(8,128)(2,1)S(1)} collective-permute-done((bf16[96,3072]{1,0:T(8,128)(2,1)S(1)}, bf16[96,3072]{1,0:T(8,128)(2,1)S(1)}, u32[]{:S(2)}, u32[]{:S(2)}) %collective-permute-start.20) | collective-permute-done | bytes 589856 | tf_op jit(solution)/shard_map/ppermute | solution.py:37
  74.2 1.5 %collective-permute-done.19 = bf16[32,3072]{1,0:T(8,128)(2,1)S(1)} collective-permute-done((bf16[32,3072]{1,0:T(8,128)(2,1)S(1)}, bf16[32,3072]{1,0:T(8,128)(2,1)S(1)}, u32[]{:S(2)}, u32[]{:S(2)}) %collective-permute-start.19) | collective-permute-done | bytes 196640 | tf_op jit(solution)/shard_map/ppermute | solution.py:17
  76.2 1.7 %collective-permute-start.22 = (bf16[32,3072]{1,0:T(8,128)(2,1)S(1)}, bf16[32,3072]{1,0:T(8,128)(2,1)S(1)}, u32[]{:S(2)}, u32[]{:S(2)}) collective-permute-start(bf16[32,3072]{1,0:T(8,128)(2,1)S(1)} %get-tuple-element.116), channel_id=1, source_target_pairs={{0,1},{1,2},{2,3},{3,4},{4,5},{5,6},{6,7},{7,0},{8,9},{9,10},{10,1... | collective-permute-start | bytes 589832 | tf_op jit(solution)/shard_map/ppermute | solution.py:17
  77.9 3.6 %collective-permute-done.21 = bf16[32,3072]{1,0:T(8,128)(2,1)S(1)} collective-permute-done((bf16[32,3072]{1,0:T(8,128)(2,1)S(1)}, bf16[32,3072]{1,0:T(8,128)(2,1)S(1)}, u32[]{:S(2)}, u32[]{:S(2)}) %collective-permute-start.21) | collective-permute-done | bytes 196640 | tf_op jit(solution)/shard_map/ppermute | solution.py:17
  81.5 1.5 %collective-permute-done.22 = bf16[32,3072]{1,0:T(8,128)(2,1)S(1)} collective-permute-done((bf16[32,3072]{1,0:T(8,128)(2,1)S(1)}, bf16[32,3072]{1,0:T(8,128)(2,1)S(1)}, u32[]{:S(2)}, u32[]{:S(2)}) %collective-permute-start.22) | collective-permute-done | bytes 196640 | tf_op jit(solution)/shard_map/ppermute | solution.py:17
  84.2 4.7 %collective-permute-done.23 = bf16[32,3072]{1,0:T(8,128)(2,1)S(1)} collective-permute-done((bf16[32,3072]{1,0:T(8,128)(2,1)S(1)}, bf16[32,3072]{1,0:T(8,128)(2,1)S(1)}, u32[]{:S(2)}, u32[]{:S(2)}) %collective-permute-start.23) | collective-permute-done | bytes 196640 | tf_op jit(solution)/shard_map/ppermute | solution.py:41
  (51 shorter events, 13.2 us)
Async XLA Ops:
  1.4 6.9 %collective-permute-start = (bf16[32,3072]{1,0:T(8,128)(2,1)S(1)}, bf16[32,3072]{1,0:T(8,128)(2,1)S(1)}, u32[]{:S(2)}, u32[]{:S(2)}) collective-permute-start(bf16[32,3072]{1,0:T(8,128)(2,1)S(1)} %convolution_convert_fusion.1), channel_id=1, source_target_pairs={{0,1},{1,0},{2,3},{3,2},{4,5},{5,4},{6,7},{7,6},{8,9},{9,8},{10,11... | collective-permute-start | bytes 589832 | tf_op jit(solution)/shard_map/ppermute | solution.py:41
  8.3 9.6 %collective-permute-start.2 = (bf16[32,3072]{1,0:T(8,128)(2,1)S(1)}, bf16[32,3072]{1,0:T(8,128)(2,1)S(1)}, u32[]{:S(2)}, u32[]{:S(2)}) collective-permute-start(bf16[32,3072]{1,0:T(8,128)(2,1)S(1)} %add.62.refs_0_), channel_id=1, source_target_pairs={{0,7},{1,0},{2,1},{3,2},{4,3},{5,4},{6,5},{7,6},{8,15},{9,8},{10,9... | collective-permute-start | bytes 589832 | tf_op jit(solution)/shard_map/ppermute | solution.py:17
  14.1 7.1 %collective-permute-start.1 = (bf16[32,3072]{1,0:T(8,128)(2,1)S(1)}, bf16[32,3072]{1,0:T(8,128)(2,1)S(1)}, u32[]{:S(2)}, u32[]{:S(2)}) collective-permute-start(bf16[32,3072]{1,0:T(8,128)(2,1)S(1)} %add.62.refs_0_), channel_id=1, source_target_pairs={{0,1},{1,2},{2,3},{3,4},{4,5},{5,6},{6,7},{7,0},{8,9},{9,10},{10,1... | collective-permute-start | bytes 589832 | tf_op jit(solution)/shard_map/ppermute | solution.py:17
  17.9 6.5 %collective-permute-start.5 = (bf16[32,3072]{1,0:T(8,128)(2,1)S(1)}, bf16[32,3072]{1,0:T(8,128)(2,1)S(1)}, u32[]{:S(2)}, u32[]{:S(2)}) collective-permute-start(bf16[32,3072]{1,0:T(8,128)(2,1)S(1)} %collective-permute-done.2.refs_2_), channel_id=1, source_target_pairs={{0,7},{1,0},{2,1},{3,2},{4,3},{5,4},{6,5},{7,6},{8,15},{9,8},{10,9... | collective-permute-start | bytes 589832 | tf_op jit(solution)/shard_map/ppermute | solution.py:17
  21.2 6.9 %collective-permute-start.4 = (bf16[32,3072]{1,0:T(8,128)(2,1)S(1)}, bf16[32,3072]{1,0:T(8,128)(2,1)S(1)}, u32[]{:S(2)}, u32[]{:S(2)}) collective-permute-start(bf16[32,3072]{1,0:T(8,128)(2,1)S(1)} %collective-permute-done.1.refs_1_), channel_id=1, source_target_pairs={{0,1},{1,2},{2,3},{3,4},{4,5},{5,6},{6,7},{7,0},{8,9},{9,10},{10,1... | collective-permute-start | bytes 589832 | tf_op jit(solution)/shard_map/ppermute | solution.py:17
  21.3 14.7 %collective-permute-start.3 = (bf16[96,3072]{1,0:T(8,128)(2,1)S(1)}, bf16[96,3072]{1,0:T(8,128)(2,1)S(1)}, u32[]{:S(2)}, u32[]{:S(2)}) collective-permute-start(bf16[96,3072]{1,0:T(8,128)(2,1)S(1)} %pad_maximum_fusion), channel_id=1, source_target_pairs={{0,8},{16,152},{8,128},{24,16},{128,136},{144,24},{136,0},{152,144... | collective-permute-start | bytes 1769480 | tf_op jit(solution)/shard_map/ppermute | solution.py:37
  24.4 6.9 %collective-permute-start.8 = (bf16[32,3072]{1,0:T(8,128)(2,1)S(1)}, bf16[32,3072]{1,0:T(8,128)(2,1)S(1)}, u32[]{:S(2)}, u32[]{:S(2)}) collective-permute-start(bf16[32,3072]{1,0:T(8,128)(2,1)S(1)} %collective-permute-done.5.refs_4_), channel_id=1, source_target_pairs={{0,7},{1,0},{2,1},{3,2},{4,3},{5,4},{6,5},{7,6},{8,15},{9,8},{10,9... | collective-permute-start | bytes 589832 | tf_op jit(solution)/shard_map/ppermute | solution.py:17
  28.1 6.9 %collective-permute-start.7 = (bf16[32,3072]{1,0:T(8,128)(2,1)S(1)}, bf16[32,3072]{1,0:T(8,128)(2,1)S(1)}, u32[]{:S(2)}, u32[]{:S(2)}) collective-permute-start(bf16[32,3072]{1,0:T(8,128)(2,1)S(1)} %collective-permute-done.4.refs_3_), channel_id=1, source_target_pairs={{0,1},{1,2},{2,3},{3,4},{4,5},{5,6},{6,7},{7,0},{8,9},{9,10},{10,1... | collective-permute-start | bytes 589832 | tf_op jit(solution)/shard_map/ppermute | solution.py:17
  28.1 7.9 %collective-permute-start.6 = (bf16[64,3072]{1,0:T(8,128)(2,1)S(1)}, bf16[64,3072]{1,0:T(8,128)(2,1)S(1)}, u32[]{:S(2)}, u32[]{:S(2)}) collective-permute-start(bf16[64,3072]{1,0:T(8,128)(2,1)S(1)} %pad_maximum_fusion.1), channel_id=1, source_target_pairs={{0,8},{16,152},{8,128},{24,16},{128,136},{144,24},{136,0},{152,144... | collective-permute-start | bytes 1179656 | tf_op jit(solution)/shard_map/ppermute | solution.py:37
  35.0 10.4 %collective-permute-start.10 = (bf16[64,3072]{1,0:T(8,128)(2,1)S(1)}, bf16[64,3072]{1,0:T(8,128)(2,1)S(1)}, u32[]{:S(2)}, u32[]{:S(2)}) collective-permute-start(bf16[64,3072]{1,0:T(8,128)(2,1)S(1)} %pad_maximum_fusion.2), channel_id=1, source_target_pairs={{0,8},{16,152},{8,128},{24,16},{128,136},{144,24},{136,0},{152,144... | collective-permute-start | bytes 1179656 | tf_op jit(solution)/shard_map/ppermute | solution.py:37
  35.3 8.0 %collective-permute-start.11 = (bf16[32,3072]{1,0:T(8,128)(2,1)S(1)}, bf16[32,3072]{1,0:T(8,128)(2,1)S(1)}, u32[]{:S(2)}, u32[]{:S(2)}) collective-permute-start(bf16[32,3072]{1,0:T(8,128)(2,1)S(1)} %broadcast_select_fusion), channel_id=1, source_target_pairs={{0,9},{1,10},{2,11},{3,12},{4,13},{5,14},{6,15},{7,8},{16,159},{17... | collective-permute-start | bytes 589832 | tf_op jit(solution)/shard_map/ppermute | solution.py:54
  35.4 10.0 %collective-permute-start.9 = (bf16[32,3072]{1,0:T(8,128)(2,1)S(1)}, bf16[32,3072]{1,0:T(8,128)(2,1)S(1)}, u32[]{:S(2)}, u32[]{:S(2)}) collective-permute-start(bf16[32,3072]{1,0:T(8,128)(2,1)S(1)} %broadcast_select_fusion), channel_id=1, source_target_pairs={{0,1},{1,2},{2,3},{3,4},{4,5},{5,6},{6,7},{7,0},{16,23},{17,16},{1... | collective-permute-start | bytes 589832 | tf_op jit(solution)/shard_map/ppermute | solution.py:27
  46.9 12.4 %collective-permute-start.14 = (bf16[64,3072]{1,0:T(8,128)(2,1)S(1)}, bf16[64,3072]{1,0:T(8,128)(2,1)S(1)}, u32[]{:S(2)}, u32[]{:S(2)}) collective-permute-start(bf16[64,3072]{1,0:T(8,128)(2,1)S(1)} %get-tuple-element.95), channel_id=1, source_target_pairs={{0,136},{16,24},{8,0},{24,144},{128,8},{144,152},{136,128},{152,16... | collective-permute-start | bytes 1179656 | tf_op jit(solution)/shard_map/ppermute | solution.py:37
  47.9 5.7 %collective-permute-start.12 = (bf16[32,3072]{1,0:T(8,128)(2,1)S(1)}, bf16[32,3072]{1,0:T(8,128)(2,1)S(1)}, u32[]{:S(2)}, u32[]{:S(2)}) collective-permute-start(bf16[32,3072]{1,0:T(8,128)(2,1)S(1)} %get-tuple-element.93), channel_id=1, source_target_pairs={{0,7},{1,0},{2,1},{3,2},{4,3},{5,4},{6,5},{7,6},{16,17},{17,18},{1... | collective-permute-start | bytes 589832 | tf_op jit(solution)/shard_map/ppermute | solution.py:27
  47.9 11.5 %collective-permute-start.13 = (bf16[32,3072]{1,0:T(8,128)(2,1)S(1)}, bf16[32,3072]{1,0:T(8,128)(2,1)S(1)}, u32[]{:S(2)}, u32[]{:S(2)}) collective-permute-start(bf16[32,3072]{1,0:T(8,128)(2,1)S(1)} %get-tuple-element.94), channel_id=1, source_target_pairs={{0,143},{1,136},{2,137},{3,138},{4,139},{5,140},{6,141},{7,142},{1... | collective-permute-start | bytes 589832 | tf_op jit(solution)/shard_map/ppermute | solution.py:54
  48.9 13.5 %collective-permute-start.17 = (bf16[64,3072]{1,0:T(8,128)(2,1)S(1)}, bf16[64,3072]{1,0:T(8,128)(2,1)S(1)}, u32[]{:S(2)}, u32[]{:S(2)}) collective-permute-start(bf16[64,3072]{1,0:T(8,128)(2,1)S(1)} %get-tuple-element.102), channel_id=1, source_target_pairs={{0,136},{16,24},{8,0},{24,144},{128,8},{144,152},{136,128},{152,16... | collective-permute-start | bytes 1179656 | tf_op jit(solution)/shard_map/ppermute | solution.py:37
  59.6 7.0 %collective-permute-start.15 = (bf16[32,3072]{1,0:T(8,128)(2,1)S(1)}, bf16[32,3072]{1,0:T(8,128)(2,1)S(1)}, u32[]{:S(2)}, u32[]{:S(2)}) collective-permute-start(bf16[32,3072]{1,0:T(8,128)(2,1)S(1)} %get-tuple-element.100), channel_id=1, source_target_pairs={{0,7},{1,0},{2,1},{3,2},{4,3},{5,4},{6,5},{7,6},{8,15},{9,8},{10,9... | collective-permute-start | bytes 589832 | tf_op jit(solution)/shard_map/ppermute | solution.py:17
  59.7 8.2 %collective-permute-start.16 = (bf16[32,3072]{1,0:T(8,128)(2,1)S(1)}, bf16[32,3072]{1,0:T(8,128)(2,1)S(1)}, u32[]{:S(2)}, u32[]{:S(2)}) collective-permute-start(bf16[32,3072]{1,0:T(8,128)(2,1)S(1)} %get-tuple-element.101), channel_id=1, source_target_pairs={{0,1},{1,2},{2,3},{3,4},{4,5},{5,6},{6,7},{7,0},{8,9},{9,10},{10,1... | collective-permute-start | bytes 589832 | tf_op jit(solution)/shard_map/ppermute | solution.py:17
  61.7 11.1 %collective-permute-start.20 = (bf16[96,3072]{1,0:T(8,128)(2,1)S(1)}, bf16[96,3072]{1,0:T(8,128)(2,1)S(1)}, u32[]{:S(2)}, u32[]{:S(2)}) collective-permute-start(bf16[96,3072]{1,0:T(8,128)(2,1)S(1)} %get-tuple-element.109), channel_id=1, source_target_pairs={{0,136},{16,24},{8,0},{24,144},{128,8},{144,152},{136,128},{152,16... | collective-permute-start | bytes 1769480 | tf_op jit(solution)/shard_map/ppermute | solution.py:37
  68.0 6.1 %collective-permute-start.18 = (bf16[32,3072]{1,0:T(8,128)(2,1)S(1)}, bf16[32,3072]{1,0:T(8,128)(2,1)S(1)}, u32[]{:S(2)}, u32[]{:S(2)}) collective-permute-start(bf16[32,3072]{1,0:T(8,128)(2,1)S(1)} %get-tuple-element.107), channel_id=1, source_target_pairs={{0,7},{1,0},{2,1},{3,2},{4,3},{5,4},{6,5},{7,6},{8,15},{9,8},{10,9... | collective-permute-start | bytes 589832 | tf_op jit(solution)/shard_map/ppermute | solution.py:17
  68.3 7.3 %collective-permute-start.19 = (bf16[32,3072]{1,0:T(8,128)(2,1)S(1)}, bf16[32,3072]{1,0:T(8,128)(2,1)S(1)}, u32[]{:S(2)}, u32[]{:S(2)}) collective-permute-start(bf16[32,3072]{1,0:T(8,128)(2,1)S(1)} %get-tuple-element.108), channel_id=1, source_target_pairs={{0,1},{1,2},{2,3},{3,4},{4,5},{5,6},{6,7},{7,0},{8,9},{9,10},{10,1... | collective-permute-start | bytes 589832 | tf_op jit(solution)/shard_map/ppermute | solution.py:17
  75.8 5.7 %collective-permute-start.21 = (bf16[32,3072]{1,0:T(8,128)(2,1)S(1)}, bf16[32,3072]{1,0:T(8,128)(2,1)S(1)}, u32[]{:S(2)}, u32[]{:S(2)}) collective-permute-start(bf16[32,3072]{1,0:T(8,128)(2,1)S(1)} %get-tuple-element.115), channel_id=1, source_target_pairs={{0,7},{1,0},{2,1},{3,2},{4,3},{5,4},{6,5},{7,6},{8,15},{9,8},{10,9... | collective-permute-start | bytes 589832 | tf_op jit(solution)/shard_map/ppermute | solution.py:17
  76.2 6.9 %collective-permute-start.22 = (bf16[32,3072]{1,0:T(8,128)(2,1)S(1)}, bf16[32,3072]{1,0:T(8,128)(2,1)S(1)}, u32[]{:S(2)}, u32[]{:S(2)}) collective-permute-start(bf16[32,3072]{1,0:T(8,128)(2,1)S(1)} %get-tuple-element.116), channel_id=1, source_target_pairs={{0,1},{1,2},{2,3},{3,4},{4,5},{5,6},{6,7},{7,0},{8,9},{9,10},{10,1... | collective-permute-start | bytes 589832 | tf_op jit(solution)/shard_map/ppermute | solution.py:17
  83.1 5.8 %collective-permute-start.23 = (bf16[32,3072]{1,0:T(8,128)(2,1)S(1)}, bf16[32,3072]{1,0:T(8,128)(2,1)S(1)}, u32[]{:S(2)}, u32[]{:S(2)}) collective-permute-start(bf16[32,3072]{1,0:T(8,128)(2,1)S(1)} %add_convert_fusion), channel_id=1, source_target_pairs={{0,1},{1,0},{2,3},{3,2},{4,5},{5,4},{6,7},{7,6},{8,9},{9,8},{10,11... | collective-permute-start | bytes 589832 | tf_op jit(solution)/shard_map/ppermute | solution.py:41
  (4 other events, 49.7 us)

commit v4 on v3

--- a/solution.py
+++ b/solution.py
@@ -17,16 +17,6 @@
     return lax.ppermute(value, "z", [(i, (i + step) % NZ) for i in range(NZ)])
 
 
-def along_z_by_core(value, step):
-    def index(core, z):
-        return core * NZ + z
-
-    pairs = [
-        (index(core, z), index(core, (z + (step if core == 0 else -step)) % NZ)) for core in range(2) for z in range(NZ)
-    ]
-    return lax.ppermute(value, ("core", "z"), pairs)
-
-
 def along_y(value, step):
     def index(y, core):
         return ((y // 2) * 2 + core) * 2 + y % 2
@@ -46,7 +36,7 @@
         return (((y // 2) * 2 + core) * 2 + y % 2) * NZ + z
 
     pairs = [
-        (index(y, core, z), index((y + (step_y if core == 0 else -step_y)) % NY, core, (z + (step_z if core == 0 else -step_z)) % NZ))
+        (index(y, core, z), index((y + (step_y if core == 0 else -step_y)) % NY, core, (z + step_z) % NZ))
         for y in range(NY)
         for core in range(2)
         for z in range(NZ)
@@ -157,7 +147,6 @@
     arrived, kept = together((arrived, kept))
     own = arrived + kept
 
-    first = lax.axis_index("core") == 0
     up1, down1 = along_z(own, 1), along_z(own, -1)
     weights = fetch(w_gate, w_up, w_down)
     down1, weights = together((down1, weights))
@@ -165,19 +154,18 @@
     y1 = along_y(jnp.concatenate([own, up1, down1]), 1)
     up3, down3 = along_z(up2, 1), along_z(down2, -1)
     y2 = along_y(jnp.concatenate([up2, down2]), 1)
-    last = jnp.where(first, up3, down3)
-    far, y4 = along_z_by_core(last, 1), diagonal(last, 1, 1)
+    far, y4 = along_z(up3, 1), diagonal(down3, 1, -1)
     y3 = along_y(jnp.concatenate([up3, down3]), 1)
     y1, y2, *mine = together((y1, y2, own, up1, down1, up2, down2, up3, down3))
     *mine, o1, o2 = expert([*mine, y1, y2], *weights)
     mine, far, y3, y4 = together((mine, far, y3, y4))
     m4, o3, o4 = expert([far, y3, y4], *weights)
 
-    f, g = along_z_by_core(m4, -1), diagonal(o4, -1, -1)
+    f_down, f_up = along_z(m4, -1), diagonal(o4, -1, 1)
     b3 = along_y(o3, -1)
-    f, g, b3 = together((f, g, b3))
-    t_down = total(mine[5], b3[:half], jnp.where(first, f, 0), jnp.where(first, g, 0))
-    t_up = total(mine[6], b3[half:], jnp.where(first, 0, f), jnp.where(first, 0, g))
+    f_down, f_up, b3 = together((f_down, f_up, b3))
+    t_down = total(mine[5], b3[:half], f_down)
+    t_up = total(mine[6], b3[half:], f_up)
     t_down, t_up = together((t_down, t_up))
     b2 = along_y(o2, -1)
     f_down, f_up = along_z(t_down, -1), along_z(t_up, 1)

time: 92.1 us -> 90.6 us (0.984); the launches traced: 90.4 us -> 90.5 us
  starting transfers between devices: 25.6 us -> 30.5 us
  waiting for transfers between devices: 51.2 us -> 46.5 us
    ppermute x2 -> x0, waiting for transfers between devices: 6.03 us -> none  [along_z_by_core(): return lax.ppermute(value, ('core', 'z'), pairs)]
    ppermute x2, waiting for transfers between devices: 9.33 us -> 3.43 us  [diagonal(): return lax.ppermute(value, ('y_hi', 'core', 'y_lo', 'z'), pairs)]
    ppermute x12 -> x14, waiting for transfers between devices: 22.9 us -> 28 us  [along_z(): return lax.ppermute(value, 'z', [(i, (i + step) % NZ) for i in range(NZ)])]
    ppermute x6, waiting for transfers between devices: 3.55 us -> 5.82 us  [along_y(): return lax.ppermute(value, ('y_hi', 'core', 'y_lo'), pairs)]
    ppermute x12 -> x14, starting transfers between devices: 19.1 us -> 21.1 us  [along_z(): return lax.ppermute(value, 'z', [(i, (i + step) % NZ) for i in range(NZ)])]
    ppermute x2, starting transfers between devices: 1.08 us -> 2.93 us  [diagonal(): return lax.ppermute(value, ('y_hi', 'core', 'y_lo', 'z'), pairs)]
    ppermute x6, starting transfers between devices: 2.55 us -> 3.68 us  [along_y(): return lax.ppermute(value, ('y_hi', 'core', 'y_lo'), pairs)]
where the time goes in v4:
time: 90.6 us; the launch traced here: 90.5 us
  waiting for transfers between devices  46.5 us (51%)
  starting transfers between devices  30.5 us (34%)
  Pallas kernels  9.11 us (10%)
  other arithmetic  2.53 us (3%)
  matrix products  1.27 us (1%)
    ppermute x14, waiting for transfers between devices, along_z(): return lax.ppermute(value, 'z', [(i, (i + step) % NZ) for i in range(NZ)])  28 us
    ppermute x14, starting transfers between devices, along_z(): return lax.ppermute(value, 'z', [(i, (i + step) % NZ) for i in range(NZ)])  21.1 us
    ppermute x2, waiting for transfers between devices, swap_pair(): return lax.ppermute(value, 'z', [(i, i ^ 1) for i in range(NZ)])  9.2 us
    ppermute x6, waiting for transfers between devices, along_y(): return lax.ppermute(value, ('y_hi', 'core', 'y_lo'), pairs)  5.82 us
    pallas_call x2, Pallas kernels, expert(): pl.pallas_call(functools.partial(expert_kernel, count), out_shape=[pltpu....  5.33 us
    pallas_call x1, Pallas kernels, fetch(): pl.pallas_call(fetch_kernel, out_shape=[pltpu.VMEM(v.shape, v.dtype) for...  3.78 us
    ppermute x6, starting transfers between devices, along_y(): return lax.ppermute(value, ('y_hi', 'core', 'y_lo'), pairs)  3.68 us
    ppermute x2, waiting for transfers between devices, diagonal(): return lax.ppermute(value, ('y_hi', 'core', 'y_lo', 'z'), pairs)  3.43 us
  transfers between devices with their start and end apart: 24, of which 18 were waited for; matrix products, arithmetic and copies ran while one was open for 1% of the time, Pallas kernels for 8%

profile of v4, /device:TPU:26, one launch (start us, length us, event | category | flops | bytes accessed | tf_op | source)
XLA Modules:
  0.0 90.5 jit_solution(14498670688646003151)
XLA Ops:
  1.4 2.0 %collective-permute-start = (bf16[32,3072]{1,0:T(8,128)(2,1)S(1)}, bf16[32,3072]{1,0:T(8,128)(2,1)S(1)}, u32[]{:S(2)}, u32[]{:S(2)}) collective-permute-start(bf16[32,3072]{1,0:T(8,128)(2,1)S(1)} %convolution_convert_fusion.1), channel_id=1, source_target_pairs={{0,1},{1,0},{2,3},{3,2},{4,5},{5,4},{6,7},{7,6},{8,9},{9,8},{10,11... | collective-permute-start | bytes 589832 | tf_op jit(solution)/shard_map/ppermute | solution.py:31
  3.6 4.7 %collective-permute-done = bf16[32,3072]{1,0:T(8,128)(2,1)S(1)} collective-permute-done((bf16[32,3072]{1,0:T(8,128)(2,1)S(1)}, bf16[32,3072]{1,0:T(8,128)(2,1)S(1)}, u32[]{:S(2)}, u32[]{:S(2)}) %collective-permute-start) | collective-permute-done | bytes 196640 | tf_op jit(solution)/shard_map/ppermute | solution.py:31
  8.3 5.8 %collective-permute-start.2 = (bf16[32,3072]{1,0:T(8,128)(2,1)S(1)}, bf16[32,3072]{1,0:T(8,128)(2,1)S(1)}, u32[]{:S(2)}, u32[]{:S(2)}) collective-permute-start(bf16[32,3072]{1,0:T(8,128)(2,1)S(1)} %add.56.refs_0_), channel_id=1, source_target_pairs={{0,7},{1,0},{2,1},{3,2},{4,3},{5,4},{6,5},{7,6},{8,15},{9,8},{10,9... | collective-permute-start | bytes 589832 | tf_op jit(solution)/shard_map/ppermute | solution.py:17
  14.1 3.8 %shard_map.73 = (bf16[3072,512]{1,0:T(8,128)(2,1)S(1)}, bf16[3072,512]{1,0:T(8,128)(2,1)S(1)}, bf16[512,3072]{1,0:T(8,128)(2,1)S(1)}) custom-call(bf16[3072,512]{1,0:T(8,128)(2,1)} %refs_0_.1, bf16[3072,512]{1,0:T(8,128)(2,1)} %refs_1_.1, bf16[512,3072]{1,0:T(8,128)(2,1)} %refs_2_.1), custom_call_target="tpu_custom_call" | custom-call | bytes 9437184 | tf_op jit(solution)/shard_map/pallas_call | solution.py:81
  17.9 3.3 %collective-permute-start.5 = (bf16[32,3072]{1,0:T(8,128)(2,1)S(1)}, bf16[32,3072]{1,0:T(8,128)(2,1)S(1)}, u32[]{:S(2)}, u32[]{:S(2)}) collective-permute-start(bf16[32,3072]{1,0:T(8,128)(2,1)S(1)} %collective-permute-done.2.refs_2_), channel_id=1, source_target_pairs={{0,7},{1,0},{2,1},{3,2},{4,3},{5,4},{6,5},{7,6},{8,15},{9,8},{10,9... | collective-permute-start | bytes 589832 | tf_op jit(solution)/shard_map/ppermute | solution.py:17
  21.6 2.8 %collective-permute-done.5.refs_4_ = bf16[32,3072]{1,0:T(8,128)(2,1)S(1)} collective-permute-done((bf16[32,3072]{1,0:T(8,128)(2,1)S(1)}, bf16[32,3072]{1,0:T(8,128)(2,1)S(1)}, u32[]{:S(2)}, u32[]{:S(2)}) %collective-permute-start.5) | collective-permute-done | bytes 196640 | tf_op jit(solution)/shard_map/ppermute | solution.py:17
  24.4 3.7 %collective-permute-start.8 = (bf16[32,3072]{1,0:T(8,128)(2,1)S(1)}, bf16[32,3072]{1,0:T(8,128)(2,1)S(1)}, u32[]{:S(2)}, u32[]{:S(2)}) collective-permute-start(bf16[32,3072]{1,0:T(8,128)(2,1)S(1)} %collective-permute-done.5.refs_4_), channel_id=1, source_target_pairs={{0,7},{1,0},{2,1},{3,2},{4,3},{5,4},{6,5},{7,6},{8,15},{9,8},{10,9... | collective-permute-start | bytes 589832 | tf_op jit(solution)/shard_map/ppermute | solution.py:17
  28.4 2.9 %collective-permute-done.8.refs_6_ = bf16[32,3072]{1,0:T(8,128)(2,1)S(1)} collective-permute-done((bf16[32,3072]{1,0:T(8,128)(2,1)S(1)}, bf16[32,3072]{1,0:T(8,128)(2,1)S(1)}, u32[]{:S(2)}, u32[]{:S(2)}) %collective-permute-start.8) | collective-permute-done | bytes 196640 | tf_op jit(solution)/shard_map/ppermute | solution.py:17
  31.3 3.7 %collective-permute-done.7.refs_5_ = bf16[32,3072]{1,0:T(8,128)(2,1)S(1)} collective-permute-done((bf16[32,3072]{1,0:T(8,128)(2,1)S(1)}, bf16[32,3072]{1,0:T(8,128)(2,1)S(1)}, u32[]{:S(2)}, u32[]{:S(2)}) %collective-permute-start.7) | collective-permute-done | bytes 196640 | tf_op jit(solution)/shard_map/ppermute | solution.py:17
  36.3 2.0 %collective-permute-start.9 = (bf16[32,3072]{1,0:T(8,128)(2,1)S(1)}, bf16[32,3072]{1,0:T(8,128)(2,1)S(1)}, u32[]{:S(2)}, u32[]{:S(2)}) collective-permute-start(bf16[32,3072]{1,0:T(8,128)(2,1)S(1)} %collective-permute-done.7.refs_5_), channel_id=1, source_target_pairs={{0,1},{1,2},{2,3},{3,4},{4,5},{5,6},{6,7},{7,0},{8,9},{9,10},{10,1... | collective-permute-start | bytes 589832 | tf_op jit(solution)/shard_map/ppermute | solution.py:17
  38.4 3.8 %shard_map.74 = (bf16[32,3072]{1,0:T(8,128)(2,1)S(1)}, bf16[32,3072]{1,0:T(8,128)(2,1)S(1)}, bf16[32,3072]{1,0:T(8,128)(2,1)S(1)}, bf16[32,3072]{1,0:T(8,128)(2,...) custom-call(bf16[32,3072]{1,0:T(8,128)(2,1)S(1)} %add.56.refs_0_, ...), custom_call_target="tpu_custom_call" | custom-call | flops 3623878656 | bytes 9437184 | tf_op jit(solution)/shard_map/pallas_call | solution.py:100
  43.2 1.8 %collective-permute-done.10.refs_1_ = bf16[64,3072]{1,0:T(8,128)(2,1)S(1)} collective-permute-done((bf16[64,3072]{1,0:T(8,128)(2,1)S(1)}, bf16[64,3072]{1,0:T(8,128)(2,1)S(1)}, u32[]{:S(2)}, u32[]{:S(2)}) %collective-permute-start.10) | collective-permute-done | bytes 393248 | tf_op jit(solution)/shard_map/ppermute | solution.py:27
  48.1 1.9 %collective-permute-start.13 = (bf16[32,3072]{1,0:T(8,128)(2,1)S(1)}, bf16[32,3072]{1,0:T(8,128)(2,1)S(1)}, u32[]{:S(2)}, u32[]{:S(2)}) collective-permute-start(bf16[32,3072]{1,0:T(8,128)(2,1)S(1)} %get-tuple-element.94), channel_id=1, source_target_pairs={{0,137},{1,138},{2,139},{3,140},{4,141},{5,142},{6,143},{7,136},{1... | collective-permute-start | bytes 589832 | tf_op jit(solution)/shard_map/ppermute | solution.py:44
  50.9 2.9 %collective-permute-done.12 = bf16[32,3072]{1,0:T(8,128)(2,1)S(1)} collective-permute-done((bf16[32,3072]{1,0:T(8,128)(2,1)S(1)}, bf16[32,3072]{1,0:T(8,128)(2,1)S(1)}, u32[]{:S(2)}, u32[]{:S(2)}) %collective-permute-start.12) | collective-permute-done | bytes 196640 | tf_op jit(solution)/shard_map/ppermute | solution.py:17
  53.7 3.4 %collective-permute-done.13 = bf16[32,3072]{1,0:T(8,128)(2,1)S(1)} collective-permute-done((bf16[32,3072]{1,0:T(8,128)(2,1)S(1)}, bf16[32,3072]{1,0:T(8,128)(2,1)S(1)}, u32[]{:S(2)}, u32[]{:S(2)}) %collective-permute-start.13) | collective-permute-done | bytes 196640 | tf_op jit(solution)/shard_map/ppermute | solution.py:44
  60.2 1.6 %collective-permute-done.17 = bf16[64,3072]{1,0:T(8,128)(2,1)S(1)} collective-permute-done((bf16[64,3072]{1,0:T(8,128)(2,1)S(1)}, bf16[64,3072]{1,0:T(8,128)(2,1)S(1)}, u32[]{:S(2)}, u32[]{:S(2)}) %collective-permute-start.17) | collective-permute-done | bytes 393248 | tf_op jit(solution)/shard_map/ppermute | solution.py:27
  61.9 2.6 %collective-permute-done.15 = bf16[32,3072]{1,0:T(8,128)(2,1)S(1)} collective-permute-done((bf16[32,3072]{1,0:T(8,128)(2,1)S(1)}, bf16[32,3072]{1,0:T(8,128)(2,1)S(1)}, u32[]{:S(2)}, u32[]{:S(2)}) %collective-permute-start.15) | collective-permute-done | bytes 196640 | tf_op jit(solution)/shard_map/ppermute | solution.py:17
  64.5 2.3 %collective-permute-done.16 = bf16[32,3072]{1,0:T(8,128)(2,1)S(1)} collective-permute-done((bf16[32,3072]{1,0:T(8,128)(2,1)S(1)}, bf16[32,3072]{1,0:T(8,128)(2,1)S(1)}, u32[]{:S(2)}, u32[]{:S(2)}) %collective-permute-start.16) | collective-permute-done | bytes 196640 | tf_op jit(solution)/shard_map/ppermute | solution.py:17
  67.0 2.0 %collective-permute-start.19 = (bf16[32,3072]{1,0:T(8,128)(2,1)S(1)}, bf16[32,3072]{1,0:T(8,128)(2,1)S(1)}, u32[]{:S(2)}, u32[]{:S(2)}) collective-permute-start(bf16[32,3072]{1,0:T(8,128)(2,1)S(1)} %get-tuple-element.108), channel_id=1, source_target_pairs={{0,1},{1,2},{2,3},{3,4},{4,5},{5,6},{6,7},{7,0},{8,9},{9,10},{10,1... | collective-permute-start | bytes 589832 | tf_op jit(solution)/shard_map/ppermute | solution.py:17
  69.0 1.9 %collective-permute-done.20 = bf16[96,3072]{1,0:T(8,128)(2,1)S(1)} collective-permute-done((bf16[96,3072]{1,0:T(8,128)(2,1)S(1)}, bf16[96,3072]{1,0:T(8,128)(2,1)S(1)}, u32[]{:S(2)}, u32[]{:S(2)}) %collective-permute-start.20) | collective-permute-done | bytes 589856 | tf_op jit(solution)/shard_map/ppermute | solution.py:27
  71.0 3.6 %collective-permute-done.18 = bf16[32,3072]{1,0:T(8,128)(2,1)S(1)} collective-permute-done((bf16[32,3072]{1,0:T(8,128)(2,1)S(1)}, bf16[32,3072]{1,0:T(8,128)(2,1)S(1)}, u32[]{:S(2)}, u32[]{:S(2)}) %collective-permute-start.18) | collective-permute-done | bytes 196640 | tf_op jit(solution)/shard_map/ppermute | solution.py:17
  76.2 1.9 %collective-permute-start.22 = (bf16[32,3072]{1,0:T(8,128)(2,1)S(1)}, bf16[32,3072]{1,0:T(8,128)(2,1)S(1)}, u32[]{:S(2)}, u32[]{:S(2)}) collective-permute-start(bf16[32,3072]{1,0:T(8,128)(2,1)S(1)} %get-tuple-element.116), channel_id=1, source_target_pairs={{0,1},{1,2},{2,3},{3,4},{4,5},{5,6},{6,7},{7,0},{8,9},{9,10},{10,1... | collective-permute-start | bytes 589832 | tf_op jit(solution)/shard_map/ppermute | solution.py:17
  78.1 4.6 %collective-permute-done.21 = bf16[32,3072]{1,0:T(8,128)(2,1)S(1)} collective-permute-done((bf16[32,3072]{1,0:T(8,128)(2,1)S(1)}, bf16[32,3072]{1,0:T(8,128)(2,1)S(1)}, u32[]{:S(2)}, u32[]{:S(2)}) %collective-permute-start.21) | collective-permute-done | bytes 196640 | tf_op jit(solution)/shard_map/ppermute | solution.py:17
  84.4 4.5 %collective-permute-done.23 = bf16[32,3072]{1,0:T(8,128)(2,1)S(1)} collective-permute-done((bf16[32,3072]{1,0:T(8,128)(2,1)S(1)}, bf16[32,3072]{1,0:T(8,128)(2,1)S(1)}, u32[]{:S(2)}, u32[]{:S(2)}) %collective-permute-start.23) | collective-permute-done | bytes 196640 | tf_op jit(solution)/shard_map/ppermute | solution.py:31
  (50 shorter events, 16.7 us)
Async XLA Ops:
  1.4 6.9 %collective-permute-start = (bf16[32,3072]{1,0:T(8,128)(2,1)S(1)}, bf16[32,3072]{1,0:T(8,128)(2,1)S(1)}, u32[]{:S(2)}, u32[]{:S(2)}) collective-permute-start(bf16[32,3072]{1,0:T(8,128)(2,1)S(1)} %convolution_convert_fusion.1), channel_id=1, source_target_pairs={{0,1},{1,0},{2,3},{3,2},{4,5},{5,4},{6,7},{7,6},{8,9},{9,8},{10,11... | collective-permute-start | bytes 589832 | tf_op jit(solution)/shard_map/ppermute | solution.py:31
  8.3 9.6 %collective-permute-start.2 = (bf16[32,3072]{1,0:T(8,128)(2,1)S(1)}, bf16[32,3072]{1,0:T(8,128)(2,1)S(1)}, u32[]{:S(2)}, u32[]{:S(2)}) collective-permute-start(bf16[32,3072]{1,0:T(8,128)(2,1)S(1)} %add.56.refs_0_), channel_id=1, source_target_pairs={{0,7},{1,0},{2,1},{3,2},{4,3},{5,4},{6,5},{7,6},{8,15},{9,8},{10,9... | collective-permute-start | bytes 589832 | tf_op jit(solution)/shard_map/ppermute | solution.py:17
  14.1 7.1 %collective-permute-start.1 = (bf16[32,3072]{1,0:T(8,128)(2,1)S(1)}, bf16[32,3072]{1,0:T(8,128)(2,1)S(1)}, u32[]{:S(2)}, u32[]{:S(2)}) collective-permute-start(bf16[32,3072]{1,0:T(8,128)(2,1)S(1)} %add.56.refs_0_), channel_id=1, source_target_pairs={{0,1},{1,2},{2,3},{3,4},{4,5},{5,6},{6,7},{7,0},{8,9},{9,10},{10,1... | collective-permute-start | bytes 589832 | tf_op jit(solution)/shard_map/ppermute | solution.py:17
  17.9 6.5 %collective-permute-start.5 = (bf16[32,3072]{1,0:T(8,128)(2,1)S(1)}, bf16[32,3072]{1,0:T(8,128)(2,1)S(1)}, u32[]{:S(2)}, u32[]{:S(2)}) collective-permute-start(bf16[32,3072]{1,0:T(8,128)(2,1)S(1)} %collective-permute-done.2.refs_2_), channel_id=1, source_target_pairs={{0,7},{1,0},{2,1},{3,2},{4,3},{5,4},{6,5},{7,6},{8,15},{9,8},{10,9... | collective-permute-start | bytes 589832 | tf_op jit(solution)/shard_map/ppermute | solution.py:17
  21.2 6.9 %collective-permute-start.4 = (bf16[32,3072]{1,0:T(8,128)(2,1)S(1)}, bf16[32,3072]{1,0:T(8,128)(2,1)S(1)}, u32[]{:S(2)}, u32[]{:S(2)}) collective-permute-start(bf16[32,3072]{1,0:T(8,128)(2,1)S(1)} %collective-permute-done.1.refs_1_), channel_id=1, source_target_pairs={{0,1},{1,2},{2,3},{3,4},{4,5},{5,6},{6,7},{7,0},{8,9},{9,10},{10,1... | collective-permute-start | bytes 589832 | tf_op jit(solution)/shard_map/ppermute | solution.py:17
  21.3 17.1 %collective-permute-start.3 = (bf16[96,3072]{1,0:T(8,128)(2,1)S(1)}, bf16[96,3072]{1,0:T(8,128)(2,1)S(1)}, u32[]{:S(2)}, u32[]{:S(2)}) collective-permute-start(bf16[96,3072]{1,0:T(8,128)(2,1)S(1)} %pad_maximum_fusion), channel_id=1, source_target_pairs={{0,8},{16,152},{8,128},{24,16},{128,136},{144,24},{136,0},{152,144... | collective-permute-start | bytes 1769480 | tf_op jit(solution)/shard_map/ppermute | solution.py:27
  24.4 6.9 %collective-permute-start.8 = (bf16[32,3072]{1,0:T(8,128)(2,1)S(1)}, bf16[32,3072]{1,0:T(8,128)(2,1)S(1)}, u32[]{:S(2)}, u32[]{:S(2)}) collective-permute-start(bf16[32,3072]{1,0:T(8,128)(2,1)S(1)} %collective-permute-done.5.refs_4_), channel_id=1, source_target_pairs={{0,7},{1,0},{2,1},{3,2},{4,3},{5,4},{6,5},{7,6},{8,15},{9,8},{10,9... | collective-permute-start | bytes 589832 | tf_op jit(solution)/shard_map/ppermute | solution.py:17
  28.1 6.9 %collective-permute-start.7 = (bf16[32,3072]{1,0:T(8,128)(2,1)S(1)}, bf16[32,3072]{1,0:T(8,128)(2,1)S(1)}, u32[]{:S(2)}, u32[]{:S(2)}) collective-permute-start(bf16[32,3072]{1,0:T(8,128)(2,1)S(1)} %collective-permute-done.4.refs_3_), channel_id=1, source_target_pairs={{0,1},{1,2},{2,3},{3,4},{4,5},{5,6},{6,7},{7,0},{8,9},{9,10},{10,1... | collective-permute-start | bytes 589832 | tf_op jit(solution)/shard_map/ppermute | solution.py:17
  28.1 10.2 %collective-permute-start.6 = (bf16[64,3072]{1,0:T(8,128)(2,1)S(1)}, bf16[64,3072]{1,0:T(8,128)(2,1)S(1)}, u32[]{:S(2)}, u32[]{:S(2)}) collective-permute-start(bf16[64,3072]{1,0:T(8,128)(2,1)S(1)} %pad_maximum_fusion.1), channel_id=1, source_target_pairs={{0,8},{16,152},{8,128},{24,16},{128,136},{144,24},{136,0},{152,144... | collective-permute-start | bytes 1179656 | tf_op jit(solution)/shard_map/ppermute | solution.py:27
  35.0 10.0 %collective-permute-start.10 = (bf16[64,3072]{1,0:T(8,128)(2,1)S(1)}, bf16[64,3072]{1,0:T(8,128)(2,1)S(1)}, u32[]{:S(2)}, u32[]{:S(2)}) collective-permute-start(bf16[64,3072]{1,0:T(8,128)(2,1)S(1)} %pad_maximum_fusion.2), channel_id=1, source_target_pairs={{0,8},{16,152},{8,128},{24,16},{128,136},{144,24},{136,0},{152,144... | collective-permute-start | bytes 1179656 | tf_op jit(solution)/shard_map/ppermute | solution.py:27
  35.3 6.9 %collective-permute-start.11 = (bf16[32,3072]{1,0:T(8,128)(2,1)S(1)}, bf16[32,3072]{1,0:T(8,128)(2,1)S(1)}, u32[]{:S(2)}, u32[]{:S(2)}) collective-permute-start(bf16[32,3072]{1,0:T(8,128)(2,1)S(1)} %collective-permute-done.8.refs_6_), channel_id=1, source_target_pairs={{0,15},{1,8},{2,9},{3,10},{4,11},{5,12},{6,13},{7,14},{16,159},{17... | collective-permute-start | bytes 589832 | tf_op jit(solution)/shard_map/ppermute | solution.py:44
  36.3 6.9 %collective-permute-start.9 = (bf16[32,3072]{1,0:T(8,128)(2,1)S(1)}, bf16[32,3072]{1,0:T(8,128)(2,1)S(1)}, u32[]{:S(2)}, u32[]{:S(2)}) collective-permute-start(bf16[32,3072]{1,0:T(8,128)(2,1)S(1)} %collective-permute-done.7.refs_5_), channel_id=1, source_target_pairs={{0,1},{1,2},{2,3},{3,4},{4,5},{5,6},{6,7},{7,0},{8,9},{9,10},{10,1... | collective-permute-start | bytes 589832 | tf_op jit(solution)/shard_map/ppermute | solution.py:17
  46.5 11.2 %collective-permute-start.14 = (bf16[64,3072]{1,0:T(8,128)(2,1)S(1)}, bf16[64,3072]{1,0:T(8,128)(2,1)S(1)}, u32[]{:S(2)}, u32[]{:S(2)}) collective-permute-start(bf16[64,3072]{1,0:T(8,128)(2,1)S(1)} %get-tuple-element.95), channel_id=1, source_target_pairs={{0,136},{16,24},{8,0},{24,144},{128,8},{144,152},{136,128},{152,16... | collective-permute-start | bytes 1179656 | tf_op jit(solution)/shard_map/ppermute | solution.py:27
  48.1 5.7 %collective-permute-start.12 = (bf16[32,3072]{1,0:T(8,128)(2,1)S(1)}, bf16[32,3072]{1,0:T(8,128)(2,1)S(1)}, u32[]{:S(2)}, u32[]{:S(2)}) collective-permute-start(bf16[32,3072]{1,0:T(8,128)(2,1)S(1)} %get-tuple-element.93), channel_id=1, source_target_pairs={{0,7},{1,0},{2,1},{3,2},{4,3},{5,4},{6,5},{7,6},{8,15},{9,8},{10,9... | collective-permute-start | bytes 589832 | tf_op jit(solution)/shard_map/ppermute | solution.py:17
  48.1 9.1 %collective-permute-start.13 = (bf16[32,3072]{1,0:T(8,128)(2,1)S(1)}, bf16[32,3072]{1,0:T(8,128)(2,1)S(1)}, u32[]{:S(2)}, u32[]{:S(2)}) collective-permute-start(bf16[32,3072]{1,0:T(8,128)(2,1)S(1)} %get-tuple-element.94), channel_id=1, source_target_pairs={{0,137},{1,138},{2,139},{3,140},{4,141},{5,142},{6,143},{7,136},{1... | collective-permute-start | bytes 589832 | tf_op jit(solution)/shard_map/ppermute | solution.py:44
  50.0 11.9 %collective-permute-start.17 = (bf16[64,3072]{1,0:T(8,128)(2,1)S(1)}, bf16[64,3072]{1,0:T(8,128)(2,1)S(1)}, u32[]{:S(2)}, u32[]{:S(2)}) collective-permute-start(bf16[64,3072]{1,0:T(8,128)(2,1)S(1)} %get-tuple-element.102), channel_id=1, source_target_pairs={{0,136},{16,24},{8,0},{24,144},{128,8},{144,152},{136,128},{152,16... | collective-permute-start | bytes 1179656 | tf_op jit(solution)/shard_map/ppermute | solution.py:27
  57.8 6.7 %collective-permute-start.15 = (bf16[32,3072]{1,0:T(8,128)(2,1)S(1)}, bf16[32,3072]{1,0:T(8,128)(2,1)S(1)}, u32[]{:S(2)}, u32[]{:S(2)}) collective-permute-start(bf16[32,3072]{1,0:T(8,128)(2,1)S(1)} %get-tuple-element.100), channel_id=1, source_target_pairs={{0,7},{1,0},{2,1},{3,2},{4,3},{5,4},{6,5},{7,6},{8,15},{9,8},{10,9... | collective-permute-start | bytes 589832 | tf_op jit(solution)/shard_map/ppermute | solution.py:17
  58.4 8.4 %collective-permute-start.16 = (bf16[32,3072]{1,0:T(8,128)(2,1)S(1)}, bf16[32,3072]{1,0:T(8,128)(2,1)S(1)}, u32[]{:S(2)}, u32[]{:S(2)}) collective-permute-start(bf16[32,3072]{1,0:T(8,128)(2,1)S(1)} %get-tuple-element.101), channel_id=1, source_target_pairs={{0,1},{1,2},{2,3},{3,4},{4,5},{5,6},{6,7},{7,0},{8,9},{9,10},{10,1... | collective-permute-start | bytes 589832 | tf_op jit(solution)/shard_map/ppermute | solution.py:17
  59.9 11.1 %collective-permute-start.20 = (bf16[96,3072]{1,0:T(8,128)(2,1)S(1)}, bf16[96,3072]{1,0:T(8,128)(2,1)S(1)}, u32[]{:S(2)}, u32[]{:S(2)}) collective-permute-start(bf16[96,3072]{1,0:T(8,128)(2,1)S(1)} %get-tuple-element.109), channel_id=1, source_target_pairs={{0,136},{16,24},{8,0},{24,144},{128,8},{144,152},{136,128},{152,16... | collective-permute-start | bytes 1769480 | tf_op jit(solution)/shard_map/ppermute | solution.py:27
  66.9 7.6 %collective-permute-start.18 = (bf16[32,3072]{1,0:T(8,128)(2,1)S(1)}, bf16[32,3072]{1,0:T(8,128)(2,1)S(1)}, u32[]{:S(2)}, u32[]{:S(2)}) collective-permute-start(bf16[32,3072]{1,0:T(8,128)(2,1)S(1)} %get-tuple-element.107), channel_id=1, source_target_pairs={{0,7},{1,0},{2,1},{3,2},{4,3},{5,4},{6,5},{7,6},{8,15},{9,8},{10,9... | collective-permute-start | bytes 589832 | tf_op jit(solution)/shard_map/ppermute | solution.py:17
  67.0 8.8 %collective-permute-start.19 = (bf16[32,3072]{1,0:T(8,128)(2,1)S(1)}, bf16[32,3072]{1,0:T(8,128)(2,1)S(1)}, u32[]{:S(2)}, u32[]{:S(2)}) collective-permute-start(bf16[32,3072]{1,0:T(8,128)(2,1)S(1)} %get-tuple-element.108), channel_id=1, source_target_pairs={{0,1},{1,2},{2,3},{3,4},{4,5},{5,6},{6,7},{7,0},{8,9},{9,10},{10,1... | collective-permute-start | bytes 589832 | tf_op jit(solution)/shard_map/ppermute | solution.py:17
  76.0 6.7 %collective-permute-start.21 = (bf16[32,3072]{1,0:T(8,128)(2,1)S(1)}, bf16[32,3072]{1,0:T(8,128)(2,1)S(1)}, u32[]{:S(2)}, u32[]{:S(2)}) collective-permute-start(bf16[32,3072]{1,0:T(8,128)(2,1)S(1)} %get-tuple-element.115), channel_id=1, source_target_pairs={{0,7},{1,0},{2,1},{3,2},{4,3},{5,4},{6,5},{7,6},{8,15},{9,8},{10,9... | collective-permute-start | bytes 589832 | tf_op jit(solution)/shard_map/ppermute | solution.py:17
  76.2 6.9 %collective-permute-start.22 = (bf16[32,3072]{1,0:T(8,128)(2,1)S(1)}, bf16[32,3072]{1,0:T(8,128)(2,1)S(1)}, u32[]{:S(2)}, u32[]{:S(2)}) collective-permute-start(bf16[32,3072]{1,0:T(8,128)(2,1)S(1)} %get-tuple-element.116), channel_id=1, source_target_pairs={{0,1},{1,2},{2,3},{3,4},{4,5},{5,6},{6,7},{7,0},{8,9},{9,10},{10,1... | collective-permute-start | bytes 589832 | tf_op jit(solution)/shard_map/ppermute | solution.py:17
  83.2 5.8 %collective-permute-start.23 = (bf16[32,3072]{1,0:T(8,128)(2,1)S(1)}, bf16[32,3072]{1,0:T(8,128)(2,1)S(1)}, u32[]{:S(2)}, u32[]{:S(2)}) collective-permute-start(bf16[32,3072]{1,0:T(8,128)(2,1)S(1)} %add_convert_fusion), channel_id=1, source_target_pairs={{0,1},{1,0},{2,3},{3,2},{4,5},{5,4},{6,7},{7,6},{8,9},{9,8},{10,11... | collective-permute-start | bytes 589832 | tf_op jit(solution)/shard_map/ppermute | solution.py:31
  (4 other events, 55.8 us)

commit v5 on v4

--- a/solution.py
+++ b/solution.py
@@ -115,6 +115,23 @@
     )(*operands)
 
 
+def sum_kernel(half, at, mine, back, flow, out):
+    value = mine[...].astype(jnp.float32) + back[at : at + half, :].astype(jnp.float32)
+    out[...] = (value + flow[...].astype(jnp.float32)).astype(out.dtype)
+
+
+def passed_on(mine, back, at, flow):
+    operands = [pltpu.with_memory_space_constraint(v, pltpu.VMEM) for v in (mine, back, flow)]
+    return pl.pallas_call(
+        functools.partial(sum_kernel, mine.shape[0], at),
+        out_shape=pltpu.VMEM(mine.shape, mine.dtype),
+        in_specs=[pl.BlockSpec(memory_space=pltpu.VMEM)] * 3,
+        out_specs=pl.BlockSpec(memory_space=pltpu.VMEM),
+        compiler_params=pltpu.CompilerParams(vmem_limit_bytes=2 * 1024 * 1024),
+        cost_estimate=pl.CostEstimate(flops=3 * mine.size, transcendentals=0, bytes_accessed=1024),
+    )(*operands)
+
+
 def total(*terms):
     value = terms[0].astype(jnp.float32)
     for term in terms[1:]:
@@ -166,20 +183,13 @@
     f_down, f_up, b3 = together((f_down, f_up, b3))
     t_down = total(mine[5], b3[:half], f_down)
     t_up = total(mine[6], b3[half:], f_up)
-    t_down, t_up = together((t_down, t_up))
     b2 = along_y(o2, -1)
     f_down, f_up = along_z(t_down, -1), along_z(t_up, 1)
-    f_down, f_up, b2 = together((f_down, f_up, b2))
-    t_down = total(mine[3], b2[:half], f_down)
-    t_up = total(mine[4], b2[half:], f_up)
-    t_down, t_up = together((t_down, t_up))
     b1 = along_y(o1, -1)
-    f_down, f_up = along_z(t_down, -1), along_z(t_up, 1)
-    f_down, f_up, b1 = together((f_down, f_up, b1))
-    t_down = total(mine[1], b1[half : 2 * half], f_down)
-    t_up = total(mine[2], b1[2 * half :], f_up)
-    t_down, t_up = together((t_down, t_up))
-    f_down, f_up = along_z(t_down, -1), along_z(t_up, 1)
+    f_down = along_z(passed_on(mine[3], b2, 0, f_down), -1)
+    f_up = along_z(passed_on(mine[4], b2, half, f_up), 1)
+    f_down = along_z(passed_on(mine[1], b1, half, f_down), -1)
+    f_up = along_z(passed_on(mine[2], b1, 2 * half, f_up), 1)
     down_own = total(mine[0], b1[:half], f_down, f_up)
 
     down_other = swap_pair(down_own)

time: 90.6 us -> 90.4 us (level)
  waiting for transfers between devices: 46.5 us -> 42.2 us
  starting transfers between devices: 30.5 us -> 34.6 us
    ppermute x14, waiting for transfers between devices: 28 us -> 23.8 us  [along_z(): return lax.ppermute(value, 'z', [(i, (i + step) % NZ) for i in range(NZ)])]
    ppermute x14, starting transfers between devices: 21.1 us -> 24.4 us  [along_z(): return lax.ppermute(value, 'z', [(i, (i + step) % NZ) for i in range(NZ)])]
    ppermute x6, starting transfers between devices: 3.68 us -> 5.17 us  [along_y(): return lax.ppermute(value, ('y_hi', 'core', 'y_lo'), pairs)]
  transfers between devices with their start and end apart: 24 -> 24, of which waited for: 18 -> 16; matrix products, arithmetic and copies ran while one was open for 1% -> 1% of each run, Pallas kernels for 8% -> 9%
where the time goes in v5:
time: 90.4 us; the launch traced here: 90.3 us
  waiting for transfers between devices  42.2 us (47%)
  starting transfers between devices  34.6 us (38%)
  Pallas kernels  9.4 us (10%)
  other arithmetic  2.24 us (2%)
  matrix products  1.27 us (1%)
    ppermute x14, starting transfers between devices, along_z(): return lax.ppermute(value, 'z', [(i, (i + step) % NZ) for i in range(NZ)])  24.4 us
    ppermute x14, waiting for transfers between devices, along_z(): return lax.ppermute(value, 'z', [(i, (i + step) % NZ) for i in range(NZ)])  23.8 us
    ppermute x2, waiting for transfers between devices, swap_pair(): return lax.ppermute(value, 'z', [(i, i ^ 1) for i in range(NZ)])  9.9 us
    pallas_call x2, Pallas kernels, expert(): pl.pallas_call(functools.partial(expert_kernel, count), out_shape=[pltpu....  5.33 us
    ppermute x6, starting transfers between devices, along_y(): return lax.ppermute(value, ('y_hi', 'core', 'y_lo'), pairs)  5.17 us
    ppermute x6, waiting for transfers between devices, along_y(): return lax.ppermute(value, ('y_hi', 'core', 'y_lo'), pairs)  5.02 us
    pallas_call x1, Pallas kernels, fetch(): pl.pallas_call(fetch_kernel, out_shape=[pltpu.VMEM(v.shape, v.dtype) for...  3.78 us
    ppermute x2, waiting for transfers between devices, diagonal(): return lax.ppermute(value, ('y_hi', 'core', 'y_lo', 'z'), pairs)  3.43 us
  transfers between devices with their start and end apart: 24, of which 16 were waited for; matrix products, arithmetic and copies ran while one was open for 1% of the time, Pallas kernels for 9%

profile of v5, /device:TPU:26, one launch (start us, length us, event | category | flops | bytes accessed | tf_op | source)
XLA Modules:
  0.0 90.3 jit_solution(17770878119048520745)
XLA Ops:
  1.4 2.0 %collective-permute-start = (bf16[32,3072]{1,0:T(8,128)(2,1)S(1)}, bf16[32,3072]{1,0:T(8,128)(2,1)S(1)}, u32[]{:S(2)}, u32[]{:S(2)}) collective-permute-start(bf16[32,3072]{1,0:T(8,128)(2,1)S(1)} %convolution_convert_fusion.1), channel_id=1, source_target_pairs={{0,1},{1,0},{2,3},{3,2},{4,5},{5,4},{6,7},{7,6},{8,9},{9,8},{10,11... | collective-permute-start | bytes 589832 | tf_op jit(solution)/shard_map/ppermute | solution.py:31
  3.6 4.7 %collective-permute-done = bf16[32,3072]{1,0:T(8,128)(2,1)S(1)} collective-permute-done((bf16[32,3072]{1,0:T(8,128)(2,1)S(1)}, bf16[32,3072]{1,0:T(8,128)(2,1)S(1)}, u32[]{:S(2)}, u32[]{:S(2)}) %collective-permute-start) | collective-permute-done | bytes 196640 | tf_op jit(solution)/shard_map/ppermute | solution.py:31
  8.3 5.8 %collective-permute-start.2 = (bf16[32,3072]{1,0:T(8,128)(2,1)S(1)}, bf16[32,3072]{1,0:T(8,128)(2,1)S(1)}, u32[]{:S(2)}, u32[]{:S(2)}) collective-permute-start(bf16[32,3072]{1,0:T(8,128)(2,1)S(1)} %add.32.refs_0_), channel_id=1, source_target_pairs={{0,7},{1,0},{2,1},{3,2},{4,3},{5,4},{6,5},{7,6},{8,15},{9,8},{10,9... | collective-permute-start | bytes 589832 | tf_op jit(solution)/shard_map/ppermute | solution.py:17
  14.1 3.8 %shard_map.73 = (bf16[3072,512]{1,0:T(8,128)(2,1)S(1)}, bf16[3072,512]{1,0:T(8,128)(2,1)S(1)}, bf16[512,3072]{1,0:T(8,128)(2,1)S(1)}) custom-call(bf16[3072,512]{1,0:T(8,128)(2,1)} %refs_0_.1, bf16[3072,512]{1,0:T(8,128)(2,1)} %refs_1_.1, bf16[512,3072]{1,0:T(8,128)(2,1)} %refs_2_.1), custom_call_target="tpu_custom_call" | custom-call | bytes 9437184 | tf_op jit(solution)/shard_map/pallas_call | solution.py:81
  17.9 3.3 %collective-permute-start.5 = (bf16[32,3072]{1,0:T(8,128)(2,1)S(1)}, bf16[32,3072]{1,0:T(8,128)(2,1)S(1)}, u32[]{:S(2)}, u32[]{:S(2)}) collective-permute-start(bf16[32,3072]{1,0:T(8,128)(2,1)S(1)} %collective-permute-done.2.refs_2_), channel_id=1, source_target_pairs={{0,7},{1,0},{2,1},{3,2},{4,3},{5,4},{6,5},{7,6},{8,15},{9,8},{10,9... | collective-permute-start | bytes 589832 | tf_op jit(solution)/shard_map/ppermute | solution.py:17
  21.6 2.8 %collective-permute-done.5.refs_4_ = bf16[32,3072]{1,0:T(8,128)(2,1)S(1)} collective-permute-done((bf16[32,3072]{1,0:T(8,128)(2,1)S(1)}, bf16[32,3072]{1,0:T(8,128)(2,1)S(1)}, u32[]{:S(2)}, u32[]{:S(2)}) %collective-permute-start.5) | collective-permute-done | bytes 196640 | tf_op jit(solution)/shard_map/ppermute | solution.py:17
  24.4 3.7 %collective-permute-start.8 = (bf16[32,3072]{1,0:T(8,128)(2,1)S(1)}, bf16[32,3072]{1,0:T(8,128)(2,1)S(1)}, u32[]{:S(2)}, u32[]{:S(2)}) collective-permute-start(bf16[32,3072]{1,0:T(8,128)(2,1)S(1)} %collective-permute-done.5.refs_4_), channel_id=1, source_target_pairs={{0,7},{1,0},{2,1},{3,2},{4,3},{5,4},{6,5},{7,6},{8,15},{9,8},{10,9... | collective-permute-start | bytes 589832 | tf_op jit(solution)/shard_map/ppermute | solution.py:17
  28.4 2.9 %collective-permute-done.8.refs_6_ = bf16[32,3072]{1,0:T(8,128)(2,1)S(1)} collective-permute-done((bf16[32,3072]{1,0:T(8,128)(2,1)S(1)}, bf16[32,3072]{1,0:T(8,128)(2,1)S(1)}, u32[]{:S(2)}, u32[]{:S(2)}) %collective-permute-start.8) | collective-permute-done | bytes 196640 | tf_op jit(solution)/shard_map/ppermute | solution.py:17
  31.3 3.7 %collective-permute-done.7.refs_5_ = bf16[32,3072]{1,0:T(8,128)(2,1)S(1)} collective-permute-done((bf16[32,3072]{1,0:T(8,128)(2,1)S(1)}, bf16[32,3072]{1,0:T(8,128)(2,1)S(1)}, u32[]{:S(2)}, u32[]{:S(2)}) %collective-permute-start.7) | collective-permute-done | bytes 196640 | tf_op jit(solution)/shard_map/ppermute | solution.py:17
  36.3 2.0 %collective-permute-start.9 = (bf16[32,3072]{1,0:T(8,128)(2,1)S(1)}, bf16[32,3072]{1,0:T(8,128)(2,1)S(1)}, u32[]{:S(2)}, u32[]{:S(2)}) collective-permute-start(bf16[32,3072]{1,0:T(8,128)(2,1)S(1)} %collective-permute-done.7.refs_5_), channel_id=1, source_target_pairs={{0,1},{1,2},{2,3},{3,4},{4,5},{5,6},{6,7},{7,0},{8,9},{9,10},{10,1... | collective-permute-start | bytes 589832 | tf_op jit(solution)/shard_map/ppermute | solution.py:17
  38.4 3.8 %shard_map.74 = (bf16[32,3072]{1,0:T(8,128)(2,1)S(1)}, bf16[32,3072]{1,0:T(8,128)(2,1)S(1)}, bf16[32,3072]{1,0:T(8,128)(2,1)S(1)}, bf16[32,3072]{1,0:T(8,128)(2,...) custom-call(bf16[32,3072]{1,0:T(8,128)(2,1)S(1)} %add.32.refs_0_, ...), custom_call_target="tpu_custom_call" | custom-call | flops 3623878656 | bytes 9437184 | tf_op jit(solution)/shard_map/pallas_call | solution.py:100
  43.2 1.8 %collective-permute-done.10.refs_1_ = bf16[64,3072]{1,0:T(8,128)(2,1)S(1)} collective-permute-done((bf16[64,3072]{1,0:T(8,128)(2,1)S(1)}, bf16[64,3072]{1,0:T(8,128)(2,1)S(1)}, u32[]{:S(2)}, u32[]{:S(2)}) %collective-permute-start.10) | collective-permute-done | bytes 393248 | tf_op jit(solution)/shard_map/ppermute | solution.py:27
  46.5 1.6 %collective-permute-start.16 = (bf16[64,3072]{1,0:T(8,128)(2,1)S(1)}, bf16[64,3072]{1,0:T(8,128)(2,1)S(1)}, u32[]{:S(2)}, u32[]{:S(2)}) collective-permute-start(bf16[64,3072]{1,0:T(8,128)(2,1)S(1)} %get-tuple-element.86), channel_id=1, source_target_pairs={{0,136},{16,24},{8,0},{24,144},{128,8},{144,152},{136,128},{152,16... | collective-permute-start | bytes 1179656 | tf_op jit(solution)/shard_map/ppermute | solution.py:27
  48.1 1.9 %collective-permute-start.15 = (bf16[32,3072]{1,0:T(8,128)(2,1)S(1)}, bf16[32,3072]{1,0:T(8,128)(2,1)S(1)}, u32[]{:S(2)}, u32[]{:S(2)}) collective-permute-start(bf16[32,3072]{1,0:T(8,128)(2,1)S(1)} %get-tuple-element.85), channel_id=1, source_target_pairs={{0,137},{1,138},{2,139},{3,140},{4,141},{5,142},{6,143},{7,136},{1... | collective-permute-start | bytes 589832 | tf_op jit(solution)/shard_map/ppermute | solution.py:44
  50.9 1.8 %collective-permute-start.12 = (bf16[96,3072]{1,0:T(8,128)(2,1)S(1)}, bf16[96,3072]{1,0:T(8,128)(2,1)S(1)}, u32[]{:S(2)}, u32[]{:S(2)}) collective-permute-start(bf16[96,3072]{1,0:T(8,128)(2,1)S(1)} %get-tuple-element.76), channel_id=1, source_target_pairs={{0,136},{16,24},{8,0},{24,144},{128,8},{144,152},{136,128},{152,16... | collective-permute-start | bytes 1769480 | tf_op jit(solution)/shard_map/ppermute | solution.py:27
  53.7 3.4 %collective-permute-done.15 = bf16[32,3072]{1,0:T(8,128)(2,1)S(1)} collective-permute-done((bf16[32,3072]{1,0:T(8,128)(2,1)S(1)}, bf16[32,3072]{1,0:T(8,128)(2,1)S(1)}, u32[]{:S(2)}, u32[]{:S(2)}) %collective-permute-start.15) | collective-permute-done | bytes 196640 | tf_op jit(solution)/shard_map/ppermute | solution.py:44
  59.9 2.0 %collective-permute-done.13.back = bf16[64,3072]{1,0:T(8,128)(2,1)S(1)} collective-permute-done((bf16[64,3072]{1,0:T(8,128)(2,1)S(1)}, bf16[64,3072]{1,0:T(8,128)(2,1)S(1)}, u32[]{:S(2)}, u32[]{:S(2)}) %collective-permute-start.13) | collective-permute-done | bytes 393248 | tf_op jit(solution)/shard_map/ppermute | solution.py:27
  61.9 1.7 %collective-permute-done.17.flow = bf16[32,3072]{1,0:T(8,128)(2,1)S(1)} collective-permute-done((bf16[32,3072]{1,0:T(8,128)(2,1)S(1)}, bf16[32,3072]{1,0:T(8,128)(2,1)S(1)}, u32[]{:S(2)}, u32[]{:S(2)}) %collective-permute-start.17) | collective-permute-done | bytes 196640 | tf_op jit(solution)/shard_map/ppermute | solution.py:17
  63.7 3.2 %collective-permute-start.18 = (bf16[32,3072]{1,0:T(8,128)(2,1)S(1)}, bf16[32,3072]{1,0:T(8,128)(2,1)S(1)}, u32[]{:S(2)}, u32[]{:S(2)}) collective-permute-start(bf16[32,3072]{1,0:T(8,128)(2,1)S(1)} %shard_map.76), channel_id=1, source_target_pairs={{0,7},{1,0},{2,1},{3,2},{4,3},{5,4},{6,5},{7,6},{8,15},{9,8},{10,9... | collective-permute-start | bytes 589832 | tf_op jit(solution)/shard_map/ppermute | solution.py:17
  68.2 3.8 %collective-permute-done.18.flow = bf16[32,3072]{1,0:T(8,128)(2,1)S(1)} collective-permute-done((bf16[32,3072]{1,0:T(8,128)(2,1)S(1)}, bf16[32,3072]{1,0:T(8,128)(2,1)S(1)}, u32[]{:S(2)}, u32[]{:S(2)}) %collective-permute-start.18) | collective-permute-done | bytes 196640 | tf_op jit(solution)/shard_map/ppermute | solution.py:17
  72.1 3.8 %collective-permute-start.19 = (bf16[32,3072]{1,0:T(8,128)(2,1)S(1)}, bf16[32,3072]{1,0:T(8,128)(2,1)S(1)}, u32[]{:S(2)}, u32[]{:S(2)}) collective-permute-start(bf16[32,3072]{1,0:T(8,128)(2,1)S(1)} %shard_map.77), channel_id=1, source_target_pairs={{0,7},{1,0},{2,1},{3,2},{4,3},{5,4},{6,5},{7,6},{8,15},{9,8},{10,9... | collective-permute-start | bytes 589832 | tf_op jit(solution)/shard_map/ppermute | solution.py:17
  76.1 3.0 %collective-permute-done.19 = bf16[32,3072]{1,0:T(8,128)(2,1)S(1)} collective-permute-done((bf16[32,3072]{1,0:T(8,128)(2,1)S(1)}, bf16[32,3072]{1,0:T(8,128)(2,1)S(1)}, u32[]{:S(2)}, u32[]{:S(2)}) %collective-permute-start.19) | collective-permute-done | bytes 196640 | tf_op jit(solution)/shard_map/ppermute | solution.py:17
  79.0 3.8 %collective-permute-done.22 = bf16[32,3072]{1,0:T(8,128)(2,1)S(1)} collective-permute-done((bf16[32,3072]{1,0:T(8,128)(2,1)S(1)}, bf16[32,3072]{1,0:T(8,128)(2,1)S(1)}, u32[]{:S(2)}, u32[]{:S(2)}) %collective-permute-start.22) | collective-permute-done | bytes 196640 | tf_op jit(solution)/shard_map/ppermute | solution.py:17
  83.5 5.2 %collective-permute-done.23 = bf16[32,3072]{1,0:T(8,128)(2,1)S(1)} collective-permute-done((bf16[32,3072]{1,0:T(8,128)(2,1)S(1)}, bf16[32,3072]{1,0:T(8,128)(2,1)S(1)}, u32[]{:S(2)}, u32[]{:S(2)}) %collective-permute-start.23) | collective-permute-done | bytes 196640 | tf_op jit(solution)/shard_map/ppermute | solution.py:31
  (52 shorter events, 14.6 us)
Async XLA Ops:
  1.4 6.9 %collective-permute-start = (bf16[32,3072]{1,0:T(8,128)(2,1)S(1)}, bf16[32,3072]{1,0:T(8,128)(2,1)S(1)}, u32[]{:S(2)}, u32[]{:S(2)}) collective-permute-start(bf16[32,3072]{1,0:T(8,128)(2,1)S(1)} %convolution_convert_fusion.1), channel_id=1, source_target_pairs={{0,1},{1,0},{2,3},{3,2},{4,5},{5,4},{6,7},{7,6},{8,9},{9,8},{10,11... | collective-permute-start | bytes 589832 | tf_op jit(solution)/shard_map/ppermute | solution.py:31
  8.3 9.6 %collective-permute-start.2 = (bf16[32,3072]{1,0:T(8,128)(2,1)S(1)}, bf16[32,3072]{1,0:T(8,128)(2,1)S(1)}, u32[]{:S(2)}, u32[]{:S(2)}) collective-permute-start(bf16[32,3072]{1,0:T(8,128)(2,1)S(1)} %add.32.refs_0_), channel_id=1, source_target_pairs={{0,7},{1,0},{2,1},{3,2},{4,3},{5,4},{6,5},{7,6},{8,15},{9,8},{10,9... | collective-permute-start | bytes 589832 | tf_op jit(solution)/shard_map/ppermute | solution.py:17
  14.1 7.1 %collective-permute-start.1 = (bf16[32,3072]{1,0:T(8,128)(2,1)S(1)}, bf16[32,3072]{1,0:T(8,128)(2,1)S(1)}, u32[]{:S(2)}, u32[]{:S(2)}) collective-permute-start(bf16[32,3072]{1,0:T(8,128)(2,1)S(1)} %add.32.refs_0_), channel_id=1, source_target_pairs={{0,1},{1,2},{2,3},{3,4},{4,5},{5,6},{6,7},{7,0},{8,9},{9,10},{10,1... | collective-permute-start | bytes 589832 | tf_op jit(solution)/shard_map/ppermute | solution.py:17
  17.9 6.5 %collective-permute-start.5 = (bf16[32,3072]{1,0:T(8,128)(2,1)S(1)}, bf16[32,3072]{1,0:T(8,128)(2,1)S(1)}, u32[]{:S(2)}, u32[]{:S(2)}) collective-permute-start(bf16[32,3072]{1,0:T(8,128)(2,1)S(1)} %collective-permute-done.2.refs_2_), channel_id=1, source_target_pairs={{0,7},{1,0},{2,1},{3,2},{4,3},{5,4},{6,5},{7,6},{8,15},{9,8},{10,9... | collective-permute-start | bytes 589832 | tf_op jit(solution)/shard_map/ppermute | solution.py:17
  21.2 6.9 %collective-permute-start.4 = (bf16[32,3072]{1,0:T(8,128)(2,1)S(1)}, bf16[32,3072]{1,0:T(8,128)(2,1)S(1)}, u32[]{:S(2)}, u32[]{:S(2)}) collective-permute-start(bf16[32,3072]{1,0:T(8,128)(2,1)S(1)} %collective-permute-done.1.refs_1_), channel_id=1, source_target_pairs={{0,1},{1,2},{2,3},{3,4},{4,5},{5,6},{6,7},{7,0},{8,9},{9,10},{10,1... | collective-permute-start | bytes 589832 | tf_op jit(solution)/shard_map/ppermute | solution.py:17
  21.3 17.1 %collective-permute-start.3 = (bf16[96,3072]{1,0:T(8,128)(2,1)S(1)}, bf16[96,3072]{1,0:T(8,128)(2,1)S(1)}, u32[]{:S(2)}, u32[]{:S(2)}) collective-permute-start(bf16[96,3072]{1,0:T(8,128)(2,1)S(1)} %pad_maximum_fusion), channel_id=1, source_target_pairs={{0,8},{16,152},{8,128},{24,16},{128,136},{144,24},{136,0},{152,144... | collective-permute-start | bytes 1769480 | tf_op jit(solution)/shard_map/ppermute | solution.py:27
  24.4 6.9 %collective-permute-start.8 = (bf16[32,3072]{1,0:T(8,128)(2,1)S(1)}, bf16[32,3072]{1,0:T(8,128)(2,1)S(1)}, u32[]{:S(2)}, u32[]{:S(2)}) collective-permute-start(bf16[32,3072]{1,0:T(8,128)(2,1)S(1)} %collective-permute-done.5.refs_4_), channel_id=1, source_target_pairs={{0,7},{1,0},{2,1},{3,2},{4,3},{5,4},{6,5},{7,6},{8,15},{9,8},{10,9... | collective-permute-start | bytes 589832 | tf_op jit(solution)/shard_map/ppermute | solution.py:17
  28.1 6.9 %collective-permute-start.7 = (bf16[32,3072]{1,0:T(8,128)(2,1)S(1)}, bf16[32,3072]{1,0:T(8,128)(2,1)S(1)}, u32[]{:S(2)}, u32[]{:S(2)}) collective-permute-start(bf16[32,3072]{1,0:T(8,128)(2,1)S(1)} %collective-permute-done.4.refs_3_), channel_id=1, source_target_pairs={{0,1},{1,2},{2,3},{3,4},{4,5},{5,6},{6,7},{7,0},{8,9},{9,10},{10,1... | collective-permute-start | bytes 589832 | tf_op jit(solution)/shard_map/ppermute | solution.py:17
  28.1 10.2 %collective-permute-start.6 = (bf16[64,3072]{1,0:T(8,128)(2,1)S(1)}, bf16[64,3072]{1,0:T(8,128)(2,1)S(1)}, u32[]{:S(2)}, u32[]{:S(2)}) collective-permute-start(bf16[64,3072]{1,0:T(8,128)(2,1)S(1)} %pad_maximum_fusion.1), channel_id=1, source_target_pairs={{0,8},{16,152},{8,128},{24,16},{128,136},{144,24},{136,0},{152,144... | collective-permute-start | bytes 1179656 | tf_op jit(solution)/shard_map/ppermute | solution.py:27
  35.0 10.0 %collective-permute-start.10 = (bf16[64,3072]{1,0:T(8,128)(2,1)S(1)}, bf16[64,3072]{1,0:T(8,128)(2,1)S(1)}, u32[]{:S(2)}, u32[]{:S(2)}) collective-permute-start(bf16[64,3072]{1,0:T(8,128)(2,1)S(1)} %pad_maximum_fusion.2), channel_id=1, source_target_pairs={{0,8},{16,152},{8,128},{24,16},{128,136},{144,24},{136,0},{152,144... | collective-permute-start | bytes 1179656 | tf_op jit(solution)/shard_map/ppermute | solution.py:27
  35.3 6.9 %collective-permute-start.11 = (bf16[32,3072]{1,0:T(8,128)(2,1)S(1)}, bf16[32,3072]{1,0:T(8,128)(2,1)S(1)}, u32[]{:S(2)}, u32[]{:S(2)}) collective-permute-start(bf16[32,3072]{1,0:T(8,128)(2,1)S(1)} %collective-permute-done.8.refs_6_), channel_id=1, source_target_pairs={{0,15},{1,8},{2,9},{3,10},{4,11},{5,12},{6,13},{7,14},{16,159},{17... | collective-permute-start | bytes 589832 | tf_op jit(solution)/shard_map/ppermute | solution.py:44
  36.3 6.9 %collective-permute-start.9 = (bf16[32,3072]{1,0:T(8,128)(2,1)S(1)}, bf16[32,3072]{1,0:T(8,128)(2,1)S(1)}, u32[]{:S(2)}, u32[]{:S(2)}) collective-permute-start(bf16[32,3072]{1,0:T(8,128)(2,1)S(1)} %collective-permute-done.7.refs_5_), channel_id=1, source_target_pairs={{0,1},{1,2},{2,3},{3,4},{4,5},{5,6},{6,7},{7,0},{8,9},{9,10},{10,1... | collective-permute-start | bytes 589832 | tf_op jit(solution)/shard_map/ppermute | solution.py:17
  46.5 11.2 %collective-permute-start.16 = (bf16[64,3072]{1,0:T(8,128)(2,1)S(1)}, bf16[64,3072]{1,0:T(8,128)(2,1)S(1)}, u32[]{:S(2)}, u32[]{:S(2)}) collective-permute-start(bf16[64,3072]{1,0:T(8,128)(2,1)S(1)} %get-tuple-element.86), channel_id=1, source_target_pairs={{0,136},{16,24},{8,0},{24,144},{128,8},{144,152},{136,128},{152,16... | collective-permute-start | bytes 1179656 | tf_op jit(solution)/shard_map/ppermute | solution.py:27
  48.1 5.7 %collective-permute-start.14 = (bf16[32,3072]{1,0:T(8,128)(2,1)S(1)}, bf16[32,3072]{1,0:T(8,128)(2,1)S(1)}, u32[]{:S(2)}, u32[]{:S(2)}) collective-permute-start(bf16[32,3072]{1,0:T(8,128)(2,1)S(1)} %get-tuple-element.84), channel_id=1, source_target_pairs={{0,7},{1,0},{2,1},{3,2},{4,3},{5,4},{6,5},{7,6},{8,15},{9,8},{10,9... | collective-permute-start | bytes 589832 | tf_op jit(solution)/shard_map/ppermute | solution.py:17
  48.1 9.1 %collective-permute-start.15 = (bf16[32,3072]{1,0:T(8,128)(2,1)S(1)}, bf16[32,3072]{1,0:T(8,128)(2,1)S(1)}, u32[]{:S(2)}, u32[]{:S(2)}) collective-permute-start(bf16[32,3072]{1,0:T(8,128)(2,1)S(1)} %get-tuple-element.85), channel_id=1, source_target_pairs={{0,137},{1,138},{2,139},{3,140},{4,141},{5,142},{6,143},{7,136},{1... | collective-permute-start | bytes 589832 | tf_op jit(solution)/shard_map/ppermute | solution.py:44
  50.0 11.9 %collective-permute-start.13 = (bf16[64,3072]{1,0:T(8,128)(2,1)S(1)}, bf16[64,3072]{1,0:T(8,128)(2,1)S(1)}, u32[]{:S(2)}, u32[]{:S(2)}) collective-permute-start(bf16[64,3072]{1,0:T(8,128)(2,1)S(1)} %get-tuple-element.79), channel_id=1, source_target_pairs={{0,136},{16,24},{8,0},{24,144},{128,8},{144,152},{136,128},{152,16... | collective-permute-start | bytes 1179656 | tf_op jit(solution)/shard_map/ppermute | solution.py:27
  50.9 17.3 %collective-permute-start.12 = (bf16[96,3072]{1,0:T(8,128)(2,1)S(1)}, bf16[96,3072]{1,0:T(8,128)(2,1)S(1)}, u32[]{:S(2)}, u32[]{:S(2)}) collective-permute-start(bf16[96,3072]{1,0:T(8,128)(2,1)S(1)} %get-tuple-element.76), channel_id=1, source_target_pairs={{0,136},{16,24},{8,0},{24,144},{128,8},{144,152},{136,128},{152,16... | collective-permute-start | bytes 1769480 | tf_op jit(solution)/shard_map/ppermute | solution.py:27
  57.8 5.7 %collective-permute-start.17 = (bf16[32,3072]{1,0:T(8,128)(2,1)S(1)}, bf16[32,3072]{1,0:T(8,128)(2,1)S(1)}, u32[]{:S(2)}, u32[]{:S(2)}) collective-permute-start(bf16[32,3072]{1,0:T(8,128)(2,1)S(1)} %get-tuple-element.95), channel_id=1, source_target_pairs={{0,7},{1,0},{2,1},{3,2},{4,3},{5,4},{6,5},{7,6},{8,15},{9,8},{10,9... | collective-permute-start | bytes 589832 | tf_op jit(solution)/shard_map/ppermute | solution.py:17
  58.4 8.4 %collective-permute-start.20 = (bf16[32,3072]{1,0:T(8,128)(2,1)S(1)}, bf16[32,3072]{1,0:T(8,128)(2,1)S(1)}, u32[]{:S(2)}, u32[]{:S(2)}) collective-permute-start(bf16[32,3072]{1,0:T(8,128)(2,1)S(1)} %get-tuple-element.96), channel_id=1, source_target_pairs={{0,1},{1,2},{2,3},{3,4},{4,5},{5,6},{6,7},{7,0},{8,9},{9,10},{10,1... | collective-permute-start | bytes 589832 | tf_op jit(solution)/shard_map/ppermute | solution.py:17
  63.7 8.4 %collective-permute-start.18 = (bf16[32,3072]{1,0:T(8,128)(2,1)S(1)}, bf16[32,3072]{1,0:T(8,128)(2,1)S(1)}, u32[]{:S(2)}, u32[]{:S(2)}) collective-permute-start(bf16[32,3072]{1,0:T(8,128)(2,1)S(1)} %shard_map.76), channel_id=1, source_target_pairs={{0,7},{1,0},{2,1},{3,2},{4,3},{5,4},{6,5},{7,6},{8,15},{9,8},{10,9... | collective-permute-start | bytes 589832 | tf_op jit(solution)/shard_map/ppermute | solution.py:17
  66.9 9.0 %collective-permute-start.21 = (bf16[32,3072]{1,0:T(8,128)(2,1)S(1)}, bf16[32,3072]{1,0:T(8,128)(2,1)S(1)}, u32[]{:S(2)}, u32[]{:S(2)}) collective-permute-start(bf16[32,3072]{1,0:T(8,128)(2,1)S(1)} %shard_map.78), channel_id=1, source_target_pairs={{0,1},{1,2},{2,3},{3,4},{4,5},{5,6},{6,7},{7,0},{8,9},{9,10},{10,1... | collective-permute-start | bytes 589832 | tf_op jit(solution)/shard_map/ppermute | solution.py:17
  72.1 7.0 %collective-permute-start.19 = (bf16[32,3072]{1,0:T(8,128)(2,1)S(1)}, bf16[32,3072]{1,0:T(8,128)(2,1)S(1)}, u32[]{:S(2)}, u32[]{:S(2)}) collective-permute-start(bf16[32,3072]{1,0:T(8,128)(2,1)S(1)} %shard_map.77), channel_id=1, source_target_pairs={{0,7},{1,0},{2,1},{3,2},{4,3},{5,4},{6,5},{7,6},{8,15},{9,8},{10,9... | collective-permute-start | bytes 589832 | tf_op jit(solution)/shard_map/ppermute | solution.py:17
  75.9 7.0 %collective-permute-start.22 = (bf16[32,3072]{1,0:T(8,128)(2,1)S(1)}, bf16[32,3072]{1,0:T(8,128)(2,1)S(1)}, u32[]{:S(2)}, u32[]{:S(2)}) collective-permute-start(bf16[32,3072]{1,0:T(8,128)(2,1)S(1)} %shard_map.79), channel_id=1, source_target_pairs={{0,1},{1,2},{2,3},{3,4},{4,5},{5,6},{6,7},{7,0},{8,9},{9,10},{10,1... | collective-permute-start | bytes 589832 | tf_op jit(solution)/shard_map/ppermute | solution.py:17
  83.0 5.8 %collective-permute-start.23 = (bf16[32,3072]{1,0:T(8,128)(2,1)S(1)}, bf16[32,3072]{1,0:T(8,128)(2,1)S(1)}, u32[]{:S(2)}, u32[]{:S(2)}) collective-permute-start(bf16[32,3072]{1,0:T(8,128)(2,1)S(1)} %add_convert_fusion), channel_id=1, source_target_pairs={{0,1},{1,0},{2,3},{3,2},{4,5},{5,4},{6,7},{7,6},{8,9},{9,8},{10,11... | collective-permute-start | bytes 589832 | tf_op jit(solution)/shard_map/ppermute | solution.py:31
  (4 other events, 38.4 us)
